TPU v7x, 512 devices: a whole 4x8x8 slice. The times are simulated.
512 devices in a mesh: gx: 4 (over x), gy: 16 (over z, core), gz: 8 (over y).
Axes of the slice: x: 4, y: 8, z: 8, core: 2. Of those that a mesh axis runs over, the one named last changes fastest.
Arguments:
- velocity_partial: float32 [3, 32, 256, 1024], P(None, 'gx', 'gy', 'gz'), may hold values from -6 to 6
- pressure_source: float32 [32, 256, 1024], P('gx', 'gy', 'gz'), may hold values from -6 to 6
- metric: float32 [3, 32, 256, 1024], P(None, 'gx', 'gy', 'gz'), may hold values from 0.02 to 0.2
- screening: float32 [32, 256, 1024], P('gx', 'gy', 'gz'), may hold values from 0.5 to 5
- particle_coords: float32 [3, 262144], P(None, ('gx', 'gy', 'gz')), may hold values from -1 to 1
- particle_owner: int32 [262144, 1], P(('gx', 'gy', 'gz')), may hold values from 0 to 15; in each aligned block of 512 rows (0 to 511, 512 to 1023, ...) at most 128 rows name the same one
- particle_element: int32 [262144], P(('gx', 'gy', 'gz')), may hold values from 0 to 31
Outputs:
- pressure: float32 [32, 256, 1024], P('gx', 'gy', 'gz')
- particle_velocity: float32 [3, 262144], P(None, ('gx', 'gy', 'gz'))
Inputs may be any that keep to these rules, and one draw needn't show every extreme that they name: `particle_owner`: among the 512 particles of one device, at most 128 name the same owner, and on every device some owner is named by exactly 128.
All inputs are finite; a program needn't handle non-finite values.
Results may differ from a plain program's by a relative error of at most 0.0003.
Values sent between devices are 32-bit elements; how exact they have to be, the bound alone decides.
A program may use at most 128 MiB of HBM per device.

v0:
```python
import math

import jax
import jax.numpy as jnp
from jax import lax
from jax.sharding import PartitionSpec as P

ITERS = 3


def extended(cells, sides, width):
    for axis, dim in sides:
        count = lax.axis_size(axis)
        head = lax.slice_in_dim(cells, 0, width, axis=dim)
        tail = lax.slice_in_dim(cells, cells.shape[dim] - width, cells.shape[dim], axis=dim)
        cells = jnp.concatenate(
            [
                lax.ppermute(tail, axis, [(i, (i + 1) % count) for i in range(count)]),
                cells,
                lax.ppermute(head, axis, [((i + 1) % count, i) for i in range(count)]),
            ],
            axis=dim,
        )
    return cells


def gll_points():
    return [
        -1.0,
        -0.8717401485096066,
        -0.5917001814331423,
        -0.2092992179024789,
        0.2092992179024789,
        0.5917001814331423,
        0.8717401485096066,
        1.0,
    ]


def legendre_seven(point):
    before, current = (1.0, point)
    for order in range(1, 7):
        before, current = (
            current,
            ((2 * order + 1) * point * current - order * before) / (order + 1),
        )
    return current


def deriv_table():
    points = gll_points()
    legendre = [legendre_seven(value) for value in points]
    derivative = [[0.0] * 8 for row in range(8)]
    for i in range(8):
        for j in range(8):
            if i != j:
                derivative[i][j] = legendre[i] / legendre[j] / (points[i] - points[j])
    derivative[0][0] = -14.0
    derivative[7][7] = 14.0
    return derivative


def pair_sum(padded, axis):
    length = padded.shape[axis] - 2
    center = lax.slice_in_dim(padded, 1, length + 1, axis=axis)
    lower_rows = lax.slice_in_dim(padded, 0, length, axis=axis)
    upper_rows = lax.slice_in_dim(padded, 2, length + 2, axis=axis)
    position = lax.broadcasted_iota(jnp.int32, center.shape, axis) % 8
    return (
        center
        + jnp.where(position == 0, lower_rows, 0.0)
        + jnp.where(position == 7, upper_rows, 0.0)
    )


def wall_mask(padded):
    at_floor = lax.axis_index("gy") == 0
    at_ceiling = lax.axis_index("gy") == lax.axis_size("gy") - 1
    position = lax.broadcasted_iota(jnp.int32, padded.shape, 2)
    cut_floor = jnp.logical_and(position == 0, at_floor)
    cut_ceiling = jnp.logical_and(position == padded.shape[2] - 1, at_ceiling)
    return jnp.where(jnp.logical_or(cut_floor, cut_ceiling), 0.0, padded)


def assemble_local(fields):
    padded = extended(fields, (("gx", 1), ("gy", 2), ("gz", 3)), 1)
    padded = wall_mask(padded)
    return pair_sum(pair_sum(pair_sum(padded, 1), 2), 3)


def local_operator(field_in, metric, screening):
    extent_x, extent_y, extent_z = field_in.shape
    matrix = jnp.asarray(deriv_table(), dtype=jnp.float32)
    exact = lax.Precision.HIGHEST

    def along_x(values, table):
        shaped = values.reshape(extent_x // 8, 8, extent_y, extent_z)
        return jnp.einsum("ai,eiyz->eayz", table, shaped, precision=exact).reshape(
            extent_x, extent_y, extent_z
        )

    def along_y(values, table):
        shaped = values.reshape(extent_x, extent_y // 8, 8, extent_z)
        return jnp.einsum("ai,xeiz->xeaz", table, shaped, precision=exact).reshape(
            extent_x, extent_y, extent_z
        )

    def along_z(values, table):
        shaped = values.reshape(extent_x, extent_y, extent_z // 8, 8)
        return jnp.einsum("ai,xyei->xyea", table, shaped, precision=exact).reshape(
            extent_x, extent_y, extent_z
        )

    result = along_x(metric[0] * along_x(field_in, matrix), matrix.T)
    result = result + along_y(metric[1] * along_y(field_in, matrix), matrix.T)
    result = result + along_z(metric[2] * along_z(field_in, matrix), matrix.T)
    return result + screening * field_in


def share_weight(shape, y_start, y_total):
    x_place = lax.broadcasted_iota(jnp.int32, shape, 0) % 8
    x_share = jnp.where((x_place == 0) | (x_place == 7), 0.5, 1.0)
    y_global = lax.broadcasted_iota(jnp.int32, shape, 1) + y_start
    y_place = y_global % 8
    at_wall = (y_global == 0) | (y_global == y_total - 1)
    y_share = jnp.where(((y_place == 0) | (y_place == 7)) & jnp.logical_not(at_wall), 0.5, 1.0)
    z_place = lax.broadcasted_iota(jnp.int32, shape, 2) % 8
    z_share = jnp.where((z_place == 0) | (z_place == 7), 0.5, 1.0)
    return (x_share * y_share * z_share).astype(jnp.float32)


def lagrange_rows(coord):
    points = gll_points()
    basis_rows = []
    for i in range(8):
        factor = jnp.ones_like(coord)
        for m in range(8):
            if m != i:
                factor = factor * (coord - points[m]) / (points[i] - points[m])
        basis_rows.append(factor)
    return jnp.stack(basis_rows)


def sample(element_block, positions):
    exact = lax.Precision.HIGHEST
    basis_x = lagrange_rows(positions[0])
    basis_y = lagrange_rows(positions[1])
    basis_z = lagrange_rows(positions[2])
    partial_value = jnp.einsum("ncijk,kn->ncij", element_block, basis_z, precision=exact)
    partial_value = jnp.einsum("ncij,jn->nci", partial_value, basis_y, precision=exact)
    return jnp.einsum("nci,in->cn", partial_value, basis_x, precision=exact)


def squares_sum(weight, residual):
    return lax.psum(jnp.sum(weight * residual * residual), ("gx", "gy", "gz"))


def body(
    velocity_partial,
    pressure_source,
    metric,
    screening,
    particle_coords,
    particle_owner,
    particle_element,
):
    extent_x, extent_y, extent_z = pressure_source.shape
    stacked = jnp.concatenate([velocity_partial, pressure_source[None]], axis=0)
    assembled = assemble_local(stacked)
    velocity = assembled[:3]
    residual = assembled[3]
    weight = share_weight(
        residual.shape, lax.axis_index("gy") * extent_y, extent_y * lax.axis_size("gy")
    )
    element_table = velocity.reshape(3, extent_x // 8, 8, extent_y // 8, 8, extent_z // 8, 8)
    element_table = element_table.transpose(1, 3, 5, 0, 2, 4, 6).reshape(-1, 3, 8, 8, 8)
    particles = particle_element.shape[0]
    groups = lax.axis_size("gy")
    capacity = particles // 4
    owner_row = particle_owner[:, 0]
    one_hot = (owner_row[:, None] == jnp.arange(groups, dtype=jnp.int32)[None, :]).astype(jnp.int32)
    slot_rank = jnp.sum((jnp.cumsum(one_hot, axis=0) - one_hot) * one_hot, axis=1)
    slot_index = owner_row * capacity + slot_rank
    packed = jnp.concatenate([particle_coords, particle_element[None].astype(jnp.float32)], axis=0)
    send_buffer = jnp.zeros((4, groups * capacity), jnp.float32).at[:, slot_index].set(packed)
    send_buffer = send_buffer.reshape(4, groups, capacity)
    received = lax.all_to_all(send_buffer, "gy", split_axis=1, concat_axis=1, tiled=True)
    per_source = received.shape[2]
    total_slots = groups * per_source
    flattened = received.reshape(4, total_slots)
    block_size = math.gcd(total_slots, 512)
    blocks = total_slots // block_size
    positions = flattened[:3].reshape(3, blocks, block_size).transpose(1, 0, 2)
    element_ids = flattened[3].astype(jnp.int32).reshape(blocks, block_size)

    def sample_block(items):
        where_at, chosen = items
        return sample(element_table[chosen], where_at)

    values = lax.map(sample_block, (positions, element_ids))
    values = values.transpose(1, 0, 2).reshape(3, groups, per_source)
    returned = lax.all_to_all(values, "gy", split_axis=1, concat_axis=1, tiled=True)
    particle_velocity = returned.reshape(3, groups * capacity)[:, slot_index]
    pressure = jnp.zeros_like(residual)
    direction = residual
    norm_now = squares_sum(weight, residual)
    for iteration in range(ITERS):
        operator_image = assemble_local(local_operator(direction, metric, screening)[None])[0]
        curvature = lax.psum(jnp.sum(weight * direction * operator_image), ("gx", "gy", "gz"))
        step_length = norm_now / curvature
        pressure = pressure + step_length * direction
        residual = residual - step_length * operator_image
        norm_next = squares_sum(weight, residual)
        direction = residual + norm_next / norm_now * direction
        norm_now = norm_next
    return (pressure, particle_velocity)


def solution(mesh):
    in_specs = (
        P(None, "gx", "gy", "gz"),
        P("gx", "gy", "gz"),
        P(None, "gx", "gy", "gz"),
        P("gx", "gy", "gz"),
        P(None, ("gx", "gy", "gz")),
        P(("gx", "gy", "gz"), None),
        P(("gx", "gy", "gz")),
    )
    out_specs = (P("gx", "gy", "gz"), P(None, ("gx", "gy", "gz")))
    return jax.shard_map(body, mesh=mesh, in_specs=in_specs, out_specs=out_specs, check_vma=False)
```

profile of v0, /device:TPU:1, one launch (start us, length us, event | category | flops | bytes accessed | tf_op | source)
XLA Modules:
  0.0 848.8 jit_solution(14055311921409100002)
XLA Ops:
  2.5 3.9 collective-permute-start
  6.5 3.2 collective-permute-start.1
  11.4 3.8 collective-permute-start.2
  15.3 3.0 collective-permute-start.3
  19.8 2.7 collective-permute-start.4
  22.9 3.8 collective-permute-start.5
  26.9 1.2 reduce-window.6
  33.5 3.1 collective-permute-start.6
  36.6 3.8 collective-permute-start.7
  41.1 1.6 collective-permute-start.8
  42.7 3.5 collective-permute-start.9
  47.2 3.0 collective-permute-start.10
  50.2 3.6 collective-permute-start.11
  54.4 2.6 collective-permute-done.11
  58.4 104.7 %all-reduce = (f32[]{:T(128)}, f32[]{:T(128)}) all-reduce(f32[]{:T(128)} %get-tuple-element.165, f32[]{:T(128)} %get-tuple-element.164), channel_id=1, replica_groups=mesh['gx'=4,'gy'=16,'gz'=8] {'gx','gy','gz'}, use_global_device_ids=true, to_apply=%region_1.2 | all-reduce | flops 2 | bytes 16 | tf_op jit(solution)/shard_map/psum | solution.py:155
  165.4 94.9 %psum.44 = f32[]{:T(128)} all-reduce(f32[]{:T(128)} %get-tuple-element.184), channel_id=1, replica_groups=mesh['gx'=4,'gy'=16,'gz'=8] {'gx','gy','gz'}, use_global_device_ids=true, to_apply=%region_5.6 | all-reduce | flops 1 | bytes 8 | tf_op jit(solution)/shard_map/psum | solution.py:155
  265.2 1.2 fusion.10
  266.4 3.7 collective-permute-start.12
  270.1 2.8 collective-permute-start.13
  273.0 1.4 collective-permute-done.13
  274.5 1.6 collective-permute-start.14
  277.2 2.0 collective-permute-done.15
  280.0 2.9 collective-permute-start.16
  282.9 3.8 collective-permute-start.17
  287.6 2.4 scatter_custom_fusion
  291.0 6.3 all-to-all-start
  297.3 1.3 maximum_select_fusion.2
  300.5 96.7 %psum.45 = f32[]{:T(128)} all-reduce(f32[]{:T(128)} %get-tuple-element.182), channel_id=1, replica_groups=mesh['gx'=4,'gy'=16,'gz'=8] {'gx','gy','gz'}, use_global_device_ids=true, to_apply=%region_7.8 | all-reduce | flops 1 | bytes 8 | tf_op jit(solution)/shard_map/psum | solution.py:209
  399.3 94.8 %psum.46 = f32[]{:T(128)} all-reduce(f32[]{:T(128)} %fusion.78), channel_id=1, replica_groups=mesh['gx'=4,'gy'=16,'gz'=8] {'gx','gy','gz'}, use_global_device_ids=true, to_apply=%region_9.10 | all-reduce | flops 1 | bytes 8 | tf_op jit(solution)/shard_map/psum | solution.py:155
  498.0 3.7 collective-permute-start.18
  501.7 2.8 collective-permute-start.19
  505.2 3.3 reshape.2653
  508.5 2.8 copy.279
  511.4 2.1 collective-permute-start.20
  517.5 2.1 collective-permute-start.22
  519.5 4.6 collective-permute-start.23
  524.2 214.0 %while.13 = (s32[]{:T(128)}, f32[4,3,512]{2,1,0:T(4,128)}, f32[4,3,512]{2,0,1:T(4,128)}, s32[4,512]{1,0:T(4,128)S(1)}, f32[32,3,8,8,8]{4,3,2,1,0:T(8,128)S(1)}, /*index=5*/s32[]{:T(128)}, s32[]{:T(128)}, s32[]{}, s32[]{}) while((s32[]{:T(128)}, f32[4,3,512]{2,1,0:T(4,128)}, f32[4,3,512]{2,0,1:T(4,128)}, s32[4,512]{1,0:T(4,128)S(1)}, ...), condition=%wide.region_17.18_spmd, body=%wide.region_16.17_spmd.sunk | while | flops 1863684 | bytes 11594429 | solution.py:200
  524.2 1.4 multiply_bitcast_fusion.26
  526.6 18.1 %gather_fusion = f32[512,3,8,8,8]{4,3,2,1,0:T(8,128)} fusion(f32[32,3,8,8,8]{4,3,2,1,0:T(8,128)S(1)} %get-tuple-element.359, s32[1024]{0:T(1024)S(1)} %pad_clamp_fusion.3), kind=kCustom, calls=%fused_computation.clone.1 | custom fusion | bytes 6293504 | tf_op jit(solution)/shard_map/while/body/eval_jaxpr/gather | solution.py:198
  544.7 19.9 %multiply_reduce_fusion.4 = f32[512,3,8,8]{3,2,1,0:T(8,128)} fusion(f32[512,3,8,8,8]{4,3,2,1,0:T(8,128)} %gather_fusion, f32[512,8]{1,0:T(8,128)S(1)} %copy.333), kind=kLoop, calls=%fused_computation.3.clone.1 | loop fusion | flops 1474560 | bytes 3555328 | tf_op jit(solution)/shard_map/while
  564.6 4.3 copy.334
  570.4 2.2 copy.335
  573.5 2.6 fusion.157
  577.7 1.4 multiply_bitcast_fusion.26
  580.1 18.1 %gather_fusion = f32[512,3,8,8,8]{4,3,2,1,0:T(8,128)} fusion(f32[32,3,8,8,8]{4,3,2,1,0:T(8,128)S(1)} %get-tuple-element.359, s32[1024]{0:T(1024)S(1)} %pad_clamp_fusion.3), kind=kCustom, calls=%fused_computation.clone.1 | custom fusion | bytes 6293504 | tf_op jit(solution)/shard_map/while/body/eval_jaxpr/gather | solution.py:198
  598.2 19.9 %multiply_reduce_fusion.4 = f32[512,3,8,8]{3,2,1,0:T(8,128)} fusion(f32[512,3,8,8,8]{4,3,2,1,0:T(8,128)} %gather_fusion, f32[512,8]{1,0:T(8,128)S(1)} %copy.333), kind=kLoop, calls=%fused_computation.3.clone.1 | loop fusion | flops 1474560 | bytes 3555328 | tf_op jit(solution)/shard_map/while
  618.1 4.3 copy.334
  623.9 2.2 copy.335
  627.0 2.6 fusion.157
  631.2 1.4 multiply_bitcast_fusion.26
  633.6 18.1 %gather_fusion = f32[512,3,8,8,8]{4,3,2,1,0:T(8,128)} fusion(f32[32,3,8,8,8]{4,3,2,1,0:T(8,128)S(1)} %get-tuple-element.359, s32[1024]{0:T(1024)S(1)} %pad_clamp_fusion.3), kind=kCustom, calls=%fused_computation.clone.1 | custom fusion | bytes 6293504 | tf_op jit(solution)/shard_map/while/body/eval_jaxpr/gather | solution.py:198
  651.7 19.9 %multiply_reduce_fusion.4 = f32[512,3,8,8]{3,2,1,0:T(8,128)} fusion(f32[512,3,8,8,8]{4,3,2,1,0:T(8,128)} %gather_fusion, f32[512,8]{1,0:T(8,128)S(1)} %copy.333), kind=kLoop, calls=%fused_computation.3.clone.1 | loop fusion | flops 1474560 | bytes 3555328 | tf_op jit(solution)/shard_map/while
  671.6 4.3 copy.334
  677.4 2.2 copy.335
  680.5 2.6 fusion.157
  684.7 1.4 multiply_bitcast_fusion.26
  687.1 18.1 %gather_fusion = f32[512,3,8,8,8]{4,3,2,1,0:T(8,128)} fusion(f32[32,3,8,8,8]{4,3,2,1,0:T(8,128)S(1)} %get-tuple-element.359, s32[1024]{0:T(1024)S(1)} %pad_clamp_fusion.3), kind=kCustom, calls=%fused_computation.clone.1 | custom fusion | bytes 6293504 | tf_op jit(solution)/shard_map/while/body/eval_jaxpr/gather | solution.py:198
  705.1 19.9 %multiply_reduce_fusion.4 = f32[512,3,8,8]{3,2,1,0:T(8,128)} fusion(f32[512,3,8,8,8]{4,3,2,1,0:T(8,128)} %gather_fusion, f32[512,8]{1,0:T(8,128)S(1)} %copy.333), kind=kLoop, calls=%fused_computation.3.clone.1 | loop fusion | flops 1474560 | bytes 3555328 | tf_op jit(solution)/shard_map/while
  725.1 4.3 copy.334
  730.9 2.2 copy.335
  734.0 2.6 fusion.157
  738.4 1.4 maximum_select_fusion.3
  741.6 6.4 all-to-all-start.1
  748.0 96.0 %psum.47 = f32[]{:T(128)} all-reduce(f32[]{:T(128)} %fusion.73), channel_id=1, replica_groups=mesh['gx'=4,'gy'=16,'gz'=8] {'gx','gy','gz'}, use_global_device_ids=true, to_apply=%region_11.12 | all-reduce | flops 1 | bytes 8 | tf_op jit(solution)/shard_map/psum | solution.py:209
  (320 shorter events, 57.3 us)
Async XLA Ops:
  2.5 8.9 %collective-permute-start = (f32[4,1,16,128]{3,1,2,0:T(1,128)S(1)}, f32[4,1,16,128]{3,1,2,0:T(1,128)S(1)}, u32[]{:S(2)}, u32[]{:S(2)}) collective-permute-start(f32[4,1,16,128]{3,1,2,0:T(1,128)S(1)} %get-tuple-element.224), channel_id=1, source_target_pairs={{0,128},{128,256},{256,384},{384,0},{1,129},{129,257},{257,385},{3... | collective-permute-start | bytes 98312 | tf_op jit(solution)/shard_map/ppermute | solution.py:18
  6.5 4.9 collective-permute-start.1
  9.7 154.8 %copy-start.26 = (s32[8]{0:T(128)}, s32[8]{0:T(128)S(1)}, u32[]{:S(2)}) copy-start(s32[8]{0:T(128)S(1)} %get-tuple-element.250) | copy-start | bytes 100
  9.7 154.8 %copy-start.29 = (s32[8]{0:T(128)}, s32[8]{0:T(128)S(1)}, u32[]{:S(2)}) copy-start(s32[8]{0:T(128)S(1)} %get-tuple-element.251) | copy-start | bytes 100
  9.7 154.8 %copy-start.32 = (pred[8]{0:T(512)(128)(4,1)}, pred[8]{0:T(512)(128)(4,1)S(1)}, u32[]{:S(2)}) copy-start(pred[8]{0:T(512)(128)(4,1)S(1)} %compare_and_fusion.3) | copy-start | bytes 28
  9.7 47.6 %copy-start.54 = (s32[16]{0:T(128)}, s32[16]{0:T(128)S(1)}, u32[]{:S(2)}) copy-start(s32[16]{0:T(128)S(1)} %broadcast_add_fusion.25) | copy-start | bytes 196
  9.8 47.6 %copy-start.57 = (pred[16]{0:T(512)(128)(4,1)}, pred[16]{0:T(512)(128)(4,1)S(1)}, u32[]{:S(2)}) copy-start(pred[16]{0:T(512)(128)(4,1)S(1)} %compare_and_fusion) | copy-start | bytes 52
  9.8 154.8 %copy-start.15 = (s32[128]{0:T(128)}, s32[128]{0:T(128)S(1)}, u32[]{:S(2)}) copy-start(s32[128]{0:T(128)S(1)} %get-tuple-element.252) | copy-start | bytes 1540
  9.8 154.8 %copy-start.18 = (s32[128]{0:T(128)}, s32[128]{0:T(128)S(1)}, u32[]{:S(2)}) copy-start(s32[128]{0:T(128)S(1)} %get-tuple-element.253) | copy-start | bytes 1540
  11.4 46.0 %copy-start.60 = (s32[16]{0:T(128)}, s32[16]{0:T(128)S(1)}, u32[]{:S(2)}) copy-start(s32[16]{0:T(128)S(1)} %iota_and_fusion) | copy-start | bytes 196
  11.4 7.5 collective-permute-start.2
  15.3 3.8 collective-permute-start.3
  18.2 146.3 %copy-start.21 = (pred[128]{0:T(512)(128)(4,1)}, pred[128]{0:T(512)(128)(4,1)S(1)}, u32[]{:S(2)}) copy-start(pred[128]{0:T(512)(128)(4,1)S(1)} %compare_and_fusion.1) | copy-start | bytes 388
  19.8 8.3 collective-permute-start.4
  22.9 5.7 collective-permute-start.5
  26.7 30.3 %copy-start.63 = (pred[18]{0:T(512)(128)(4,1)}, pred[18]{0:T(512)(128)(4,1)S(1)}, u32[]{:S(2)}) copy-start(pred[18]{0:T(512)(128)(4,1)S(1)} %and_or_fusion) | copy-start | bytes 58
  28.0 12.3 %copy-start.9 = (s32[16,4,128]{2,0,1:T(8,128)}, s32[16,4,128]{2,0,1:T(8,128)S(1)}, u32[]{:S(2)}) copy-start(s32[16,4,128]{2,0,1:T(8,128)S(1)} %reduce-window.6) | copy-start | bytes 98308
  30.5 474.7 %copy-start = (f32[4,8,16,128]{3,1,2,0:T(8,128)}, f32[4,8,16,128]{3,1,2,0:T(8,128)S(1)}, u32[]{:S(2)}) copy-start(f32[4,8,16,128]{3,1,2,0:T(8,128)S(1)} %fusion.33) | copy-start | bytes 786436
  33.5 7.1 collective-permute-start.6
  36.6 4.6 collective-permute-start.7
  41.1 5.7 collective-permute-start.8
  42.7 4.4 collective-permute-start.9
  46.3 118.3 %copy-start.40 = (s32[16]{0:T(128)}, s32[16]{0:T(128)S(1)}, u32[]{:S(2)}) copy-start(s32[16]{0:T(128)S(1)} %get-tuple-element.246) | copy-start | bytes 196
  46.3 118.3 %copy-start.43 = (s32[16]{0:T(128)}, s32[16]{0:T(128)S(1)}, u32[]{:S(2)}) copy-start(s32[16]{0:T(128)S(1)} %get-tuple-element.247) | copy-start | bytes 196
  47.2 7.2 collective-permute-start.10
  50.2 6.8 collective-permute-start.11
  53.9 111.5 %copy-start.46 = (pred[16]{0:T(512)(128)(4,1)}, pred[16]{0:T(512)(128)(4,1)S(1)}, u32[]{:S(2)}) copy-start(pred[16]{0:T(512)(128)(4,1)S(1)} %get-tuple-element.248) | copy-start | bytes 52
  53.9 111.5 %copy-start.49 = (pred[16]{0:T(512)(128)(4,1)}, pred[16]{0:T(512)(128)(4,1)S(1)}, u32[]{:S(2)}) copy-start(pred[16]{0:T(512)(128)(4,1)S(1)} %get-tuple-element.249) | copy-start | bytes 52
  53.9 110.6 %copy-start.53 = (s32[16,5]{0,1:T(8,128)}, s32[16,5]{0,1:T(8,128)S(1)}, u32[]{:S(2)}) copy-start(s32[16,5]{0,1:T(8,128)S(1)} %reduce-window.9) | copy-start | bytes 964
  265.0 12.2 %copy-start.66 = (s32[512]{0:T(512)S(1)}, s32[512]{0:T(512)}, u32[]{:S(2)}) copy-start(s32[512]{0:T(512)} %param.18) | copy-start | bytes 6148
  265.0 21.7 %copy-start.65 = (f32[3,512]{1,0:T(4,128)S(1)}, f32[3,512]{1,0:T(4,128)}, u32[]{:S(2)}) copy-start(f32[3,512]{1,0:T(4,128)} %param.16) | copy-start | bytes 18436
  265.2 230.5 %copy-start.1 = (f32[8,16,128]{2,0,1:T(8,128)}, f32[8,16,128]{2,0,1:T(8,128)S(1)}, u32[]{:S(2)}) copy-start(f32[8,16,128]{2,0,1:T(8,128)S(1)} %fusion.89) | copy-start | bytes 196612
  266.4 6.6 collective-permute-start.12
  270.1 4.4 collective-permute-start.13
  274.5 13.1 %copy-start.14 = (f32[1,1,16,128]{3,1,2,0:T(1,128)}, f32[1,1,16,128]{3,1,2,0:T(1,128)S(1)}, u32[]{:S(2)}) copy-start(f32[1,1,16,128]{3,1,2,0:T(1,128)S(1)} %collective-permute-done.13) | copy-start | bytes 24580
  274.5 2.8 collective-permute-start.14
  276.1 3.1 collective-permute-start.15
  277.2 10.4 %copy-start.37 = (f32[1,10,1,128]{3,1,2,0:T(8,128)}, f32[1,10,1,128]{3,1,2,0:T(8,128)S(1)}, u32[]{:S(2)}) copy-start(f32[1,10,1,128]{3,1,2,0:T(8,128)S(1)} %collective-permute-done.14) | copy-start | bytes 15364
  280.0 17.3 %collective-permute-start.16 = (f32[1,10,18,1]{3,1,2,0:T(8,128)}, f32[1,10,18,1]{3,1,2,0:T(8,128)}, u32[]{:S(2)}, u32[]{:S(2)}) collective-permute-start(f32[1,10,18,1]{3,1,2,0:T(8,128)} %get-tuple-element.230), channel_id=1, source_target_pairs={{0,1},{1,2},{2,3},{3,4},{4,5},{5,6},{6,7},{7,0},{8,9},{9,10},{10,1... | collective-permute-start | bytes 2168 | tf_op jit(solution)/shard_map/ppermute | solution.py:18
  282.9 14.4 %collective-permute-start.17 = (f32[1,10,18,1]{3,1,2,0:T(8,128)}, f32[1,10,18,1]{3,1,2,0:T(8,128)}, u32[]{:S(2)}, u32[]{:S(2)}) collective-permute-start(f32[1,10,18,1]{3,1,2,0:T(8,128)} %get-tuple-element.231), channel_id=1, source_target_pairs={{1,0},{2,1},{3,2},{4,3},{5,4},{6,5},{7,6},{0,7},{9,8},{10,9},{11,1... | collective-permute-start | bytes 2168 | tf_op jit(solution)/shard_map/ppermute | solution.py:20
  290.9 8.7 %copy-start.19 = (s32[128]{0:T(128)S(1)}, s32[128]{0:T(128)}, u32[]{:S(2)}) copy-start(s32[128]{0:T(128)} %copy-done.18) | copy-start | bytes 1540
  290.9 8.7 %copy-start.22 = (pred[128]{0:T(512)(128)(4,1)S(1)}, pred[128]{0:T(512)(128)(4,1)}, u32[]{:S(2)}) copy-start(pred[128]{0:T(512)(128)(4,1)} %copy-done.21) | copy-start | bytes 388
  290.9 8.7 %copy-start.27 = (s32[8]{0:T(128)S(1)}, s32[8]{0:T(128)}, u32[]{:S(2)}) copy-start(s32[8]{0:T(128)} %copy-done.26) | copy-start | bytes 100
  290.9 8.7 %copy-start.30 = (s32[8]{0:T(128)S(1)}, s32[8]{0:T(128)}, u32[]{:S(2)}) copy-start(s32[8]{0:T(128)} %copy-done.29) | copy-start | bytes 100
  290.9 8.7 %copy-start.33 = (pred[8]{0:T(512)(128)(4,1)S(1)}, pred[8]{0:T(512)(128)(4,1)}, u32[]{:S(2)}) copy-start(pred[8]{0:T(512)(128)(4,1)} %copy-done.32) | copy-start | bytes 28
  290.9 8.7 %copy-start.41 = (s32[16]{0:T(128)S(1)}, s32[16]{0:T(128)}, u32[]{:S(2)}) copy-start(s32[16]{0:T(128)} %copy-done.40) | copy-start | bytes 196
  291.0 8.7 %copy-start.44 = (s32[16]{0:T(128)S(1)}, s32[16]{0:T(128)}, u32[]{:S(2)}) copy-start(s32[16]{0:T(128)} %copy-done.43) | copy-start | bytes 196
  291.0 222.6 %all-to-all-start = ((f32[4,16,128]{2,0,1:T(4,128)}), f32[4,16,128]{2,0,1:T(4,128)}, u32[]{:S(2)}, u32[]{:S(2)}) async-start(f32[4,16,128]{2,0,1:T(4,128)} %copy.222), calls=%async_computation | async-start | bytes 65536 | tf_op jit(solution)/shard_map/all_to_all | solution.py:187
  498.0 18.6 %copy-start.3 = (f32[1,8,16,128]{3,1,2,0:T(8,128)}, f32[1,8,16,128]{3,1,2,0:T(8,128)S(1)}, u32[]{:S(2)}) copy-start(f32[1,8,16,128]{3,1,2,0:T(8,128)S(1)} %fusion.5) | copy-start | bytes 196612
  498.0 13.3 %collective-permute-start.18 = (f32[1,1,16,128]{3,1,2,0:T(1,128)S(1)}, f32[1,1,16,128]{3,1,2,0:T(1,128)S(1)}, u32[]{:S(2)}, u32[]{:S(2)}) collective-permute-start(f32[1,1,16,128]{3,1,2,0:T(1,128)S(1)} %get-tuple-element.240), channel_id=1, source_target_pairs={{0,128},{128,256},{256,384},{384,0},{1,129},{129,257},{257,385},{3... | collective-permute-start | bytes 24584 | tf_op jit(solution)/shard_map/ppermute | solution.py:18
  501.7 9.7 %collective-permute-start.19 = (f32[1,1,16,128]{3,1,2,0:T(1,128)S(1)}, f32[1,1,16,128]{3,1,2,0:T(1,128)S(1)}, u32[]{:S(2)}, u32[]{:S(2)}) collective-permute-start(f32[1,1,16,128]{3,1,2,0:T(1,128)S(1)} %get-tuple-element.241), channel_id=1, source_target_pairs={{128,0},{256,128},{384,256},{0,384},{129,1},{257,129},{385,257},{1... | collective-permute-start | bytes 24584 | tf_op jit(solution)/shard_map/ppermute | solution.py:20
  511.4 12.8 %copy-start.12 = (f32[1,1,16,128]{3,1,2,0:T(1,128)}, f32[1,1,16,128]{3,1,2,0:T(1,128)S(1)}, u32[]{:S(2)}) copy-start(f32[1,1,16,128]{3,1,2,0:T(1,128)S(1)} %collective-permute-done.18) | copy-start | bytes 24580
  511.4 12.8 %copy-start.13 = (f32[1,1,16,128]{3,1,2,0:T(1,128)}, f32[1,1,16,128]{3,1,2,0:T(1,128)S(1)}, u32[]{:S(2)}) copy-start(f32[1,1,16,128]{3,1,2,0:T(1,128)S(1)} %collective-permute-done.19) | copy-start | bytes 24580
  511.4 4.3 collective-permute-start.20
  513.6 3.1 collective-permute-start.21
  517.5 220.9 %collective-permute-start.22 = (f32[1,10,18,1]{3,1,2,0:T(8,128)}, f32[1,10,18,1]{3,1,2,0:T(8,128)}, u32[]{:S(2)}, u32[]{:S(2)}) collective-permute-start(f32[1,10,18,1]{3,1,2,0:T(8,128)} %get-tuple-element.228), channel_id=1, source_target_pairs={{0,1},{1,2},{2,3},{3,4},{4,5},{5,6},{6,7},{7,0},{8,9},{9,10},{10,1... | collective-permute-start | bytes 2168 | tf_op jit(solution)/shard_map/ppermute | solution.py:18
  519.5 218.8 %collective-permute-start.23 = (f32[1,10,18,1]{3,1,2,0:T(8,128)}, f32[1,10,18,1]{3,1,2,0:T(8,128)}, u32[]{:S(2)}, u32[]{:S(2)}) collective-permute-start(f32[1,10,18,1]{3,1,2,0:T(8,128)} %get-tuple-element.229), channel_id=1, source_target_pairs={{1,0},{2,1},{3,2},{4,3},{5,4},{6,5},{7,6},{0,7},{9,8},{10,9},{11,1... | collective-permute-start | bytes 2168 | tf_op jit(solution)/shard_map/ppermute | solution.py:20
  524.2 20.4 %copy-start.24 = (s32[4,512]{1,0:T(4,128)}, s32[4,512]{1,0:T(4,128)S(1)}, u32[]{:S(2)}) copy-start(s32[4,512]{1,0:T(4,128)S(1)} %get-tuple-element.358) | copy-start | bytes 24580 | tf_op jit(solution)/shard_map/while
  577.7 20.4 %copy-start.24 = (s32[4,512]{1,0:T(4,128)}, s32[4,512]{1,0:T(4,128)S(1)}, u32[]{:S(2)}) copy-start(s32[4,512]{1,0:T(4,128)S(1)} %get-tuple-element.358) | copy-start | bytes 24580 | tf_op jit(solution)/shard_map/while
  631.2 20.4 %copy-start.24 = (s32[4,512]{1,0:T(4,128)}, s32[4,512]{1,0:T(4,128)S(1)}, u32[]{:S(2)}) copy-start(s32[4,512]{1,0:T(4,128)S(1)} %get-tuple-element.358) | copy-start | bytes 24580 | tf_op jit(solution)/shard_map/while
  684.7 20.4 %copy-start.24 = (s32[4,512]{1,0:T(4,128)}, s32[4,512]{1,0:T(4,128)S(1)}, u32[]{:S(2)}) copy-start(s32[4,512]{1,0:T(4,128)S(1)} %get-tuple-element.358) | copy-start | bytes 24580 | tf_op jit(solution)/shard_map/while
  738.3 106.8 %copy-start.2 = (f32[8,16,128]{2,0,1:T(8,128)S(1)}, f32[8,16,128]{2,0,1:T(8,128)}, u32[]{:S(2)}) copy-start(f32[8,16,128]{2,0,1:T(8,128)} %copy-done.1) | copy-start | bytes 196612
  740.5 106.5 %copy-start.52 = (s32[1024]{0:T(1024)S(1)}, s32[1024]{0:T(1024)}, u32[]{:S(2)}) copy-start(s32[1024]{0:T(1024)} %pad_clamp_fusion.1) | copy-start | bytes 12292
  741.6 105.1 %all-to-all-start.1 = ((f32[3,16,128]{2,0,1:T(4,128)}), f32[3,16,128]{2,0,1:T(4,128)S(1)}, u32[]{:S(2)}, u32[]{:S(2)}) async-start(f32[3,16,128]{2,0,1:T(4,128)} %bitcast.109), calls=%async_computation.1 | async-start | bytes 65536 | tf_op jit(solution)/shard_map/all_to_all | solution.py:202
  (36 other events, 168.7 us)
where the time goes:
time: 852 us; the launch traced here: 849 us
  blocking collectives  487 us (57%)
  local copies, waits for them, and re-layouts  136 us (16%)
  other arithmetic  117 us (14%)
  starting transfers between devices  82.4 us (10%)
  waiting for transfers between devices  9.64 us (1%)
  between operations  8.71 us (1%)
    psum x3, blocking collectives, squares_sum(): return lax.psum(jnp.sum(weight * residual * residual), ('gx', 'gy', 'gz'))  294 us
    psum x2, blocking collectives, body(): lax.psum(jnp.sum(weight * direction * operator_image), ('gx', 'gy', 'gz'))  193 us
    while x12, other arithmetic  93 us
    gather x4, local copies, waits for them, and re-layouts, sample_block(): return sample(element_table[chosen], where_at)  72.3 us
    ppermute x12, starting transfers between devices, extended(): lax.ppermute(head, axis, [((i + 1) % count, i) for i in range(count)])  35.4 us
    ppermute x12, starting transfers between devices, extended(): lax.ppermute(tail, axis, [(i, (i + 1) % count) for i in range(count)])  34.2 us
    while x32, local copies, waits for them, and re-layouts  27.1 us
  transfers between devices with their start and end apart: 26, of which 10 were waited for; matrix products, arithmetic and copies ran while one was open for 28% of the time, Pallas kernels for 0%

commit v1 on v0

v1 whole, which is shorter than its diff:
```python
import functools

import jax
import jax.numpy as jnp
import numpy as np
from jax import lax
from jax.experimental import pallas as pl
from jax.experimental.pallas import tpu as pltpu
from jax.sharding import PartitionSpec as P

MESH = pl.DeviceIdType.MESH
F32 = jnp.float32
BF16 = jnp.bfloat16
EXACT = lax.Precision.HIGHEST
SCALE = 1.0 / 64.0
GX, GY, GZ = 4, 16, 8
CAP = 128
FIELDS = 6


def gll_points():
    return [
        -1.0,
        -0.8717401485096066,
        -0.5917001814331423,
        -0.2092992179024789,
        0.2092992179024789,
        0.5917001814331423,
        0.8717401485096066,
        1.0,
    ]


def legendre_seven(point):
    before, current = (1.0, point)
    for order in range(1, 7):
        before, current = (
            current,
            ((2 * order + 1) * point * current - order * before) / (order + 1),
        )
    return current


def deriv_table():
    points = gll_points()
    legendre = [legendre_seven(value) for value in points]
    derivative = [[0.0] * 8 for row in range(8)]
    for i in range(8):
        for j in range(8):
            if i != j:
                derivative[i][j] = legendre[i] / legendre[j] / (points[i] - points[j])
    derivative[0][0] = -14.0
    derivative[7][7] = 14.0
    return derivative


def lagrange_scale():
    points = gll_points()
    scale = []
    for i in range(8):
        product = 1.0
        for m in range(8):
            if m != i:
                product *= points[i] - points[m]
        scale.append(1.0 / product)
    return scale


def iota(shape, dim):
    return lax.broadcasted_iota(jnp.int32, shape, dim)


def kernel(
    vel, src, met, scr, coords, owner, elem, ky, kyt, kz, kzt, lsc,
    p_out, pv_out,
    work, hxs, hx, hys, hyr, hzs, hzr, hss, hrs,
    msg, rx, rz, ry, ass, ars,
    sendp, recvp, sendv, recvv, pss, prs, vhi, vlo,
):
    gx, gy, gz = lax.axis_index("gx"), lax.axis_index("gy"), lax.axis_index("gz")

    def at_x(k):
        return (lax.rem(gx + (k + GX), GX), gy, gz)

    def at_y(k):
        return (gx, lax.rem(gy + (k + GY), GY), gz)

    def at_z(k):
        return (gx, gy, lax.rem(gz + (k + GZ), GZ))

    barrier = pltpu.get_barrier_semaphore()
    for k in range(1, GX):
        pl.semaphore_signal(barrier, inc=1, device_id=at_x(k), device_id_type=MESH)
    for k in range(1, GZ):
        pl.semaphore_signal(barrier, inc=1, device_id=at_z(k), device_id_type=MESH)
    for k in range(1, GY):
        pl.semaphore_signal(barrier, inc=1, device_id=at_y(k), device_id_type=MESH)

    sends = []

    def remote(src_ref, dst_ref, ssem, rsem, device):
        copy = pltpu.make_async_remote_copy(
            src_ref=src_ref,
            dst_ref=dst_ref,
            send_sem=ssem,
            recv_sem=rsem,
            device_id=device,
            device_id_type=MESH,
        )
        copy.start()
        sends.append(copy)
        return copy

    row_id = iota((128, 128), 0)
    lane_id = iota((128, 128), 1)
    eye = row_id == lane_id
    lane_in = lane_id % 8
    low_z = (lane_in == 0) & (lane_id > 0)
    high_z = (lane_in == 7) & (lane_id < 127)
    at_floor = gy == 0
    at_ceiling = gy == GY - 1

    def start_x(f, tail, head):
        return (
            remote(tail, hx.at[f, 0], hss.at[f, 0], hrs.at[f, 0], at_x(1)),
            remote(head, hx.at[f, 1], hss.at[f, 1], hrs.at[f, 1], at_x(-1)),
        )

    def start_image(f, field):
        work[f] = field
        hxs[f - 1, 0] = field[112:128, :]
        hxs[f - 1, 1] = field[0:16, :]
        return start_x(f, hxs.at[f - 1, 0], hxs.at[f - 1, 1])

    def mid_xy(f, copies):
        w = work.at[f]
        copies[0].wait_recv()
        w[pl.ds(0, 16), :] = w[pl.ds(0, 16), :] + hx[f, 0]
        copies[1].wait_recv()
        w[pl.ds(112, 16), :] = w[pl.ds(112, 16), :] + hx[f, 1]
        both = w[pl.ds(7, 8, stride=16), :] + w[pl.ds(8, 8, stride=16), :]
        w[pl.ds(7, 8, stride=16), :] = both
        w[pl.ds(8, 8, stride=16), :] = both
        hys[f, 0] = w[pl.ds(15, 8, stride=16), :]
        hys[f, 1] = w[pl.ds(0, 8, stride=16), :]
        return (
            remote(hys.at[f, 0], hyr.at[f, 0], hss.at[f, 2], hrs.at[f, 2], at_y(1)),
            remote(hys.at[f, 1], hyr.at[f, 1], hss.at[f, 3], hrs.at[f, 3], at_y(-1)),
        )

    def mid_yz(f, copies):
        w = work.at[f]
        copies[0].wait_recv()
        w[pl.ds(0, 8, stride=16), :] = w[pl.ds(0, 8, stride=16), :] + jnp.where(at_floor, 0.0, hyr[f, 0])
        copies[1].wait_recv()
        w[pl.ds(15, 8, stride=16), :] = w[pl.ds(15, 8, stride=16), :] + jnp.where(at_ceiling, 0.0, hyr[f, 1])
        field = w[...]
        hzs[f, 0] = jnp.sum(jnp.where(eye, field[:, 127:128], 0.0), axis=0, keepdims=True)
        hzs[f, 1] = jnp.sum(jnp.where(eye, field[:, 0:1], 0.0), axis=0, keepdims=True)
        out = (
            remote(hzs.at[f, 0], hzr.at[f, 0], hss.at[f, 4], hrs.at[f, 4], at_z(1)),
            remote(hzs.at[f, 1], hzr.at[f, 1], hss.at[f, 5], hrs.at[f, 5], at_z(-1)),
        )
        field = (
            field
            + jnp.where(low_z, pltpu.roll(field, 1, 1), 0.0)
            + jnp.where(high_z, pltpu.roll(field, 127, 1), 0.0)
        )
        return out, field

    def end_z(f, copies, field):
        copies[0].wait_recv()
        low = jnp.sum(jnp.where(eye, hzr[f, 0], 0.0), axis=1, keepdims=True)
        copies[1].wait_recv()
        high = jnp.sum(jnp.where(eye, hzr[f, 1], 0.0), axis=1, keepdims=True)
        return field + jnp.where(lane_id == 0, low, 0.0) + jnp.where(lane_id == 127, high, 0.0)

    table = deriv_table()

    def along_x(field, transposed):
        parts = [field[16 * i : 16 * i + 16, :] for i in range(8)]
        out = []
        for a in range(8):
            total = None
            for i in range(8):
                factor = table[i][a] if transposed else table[a][i]
                if factor == 0.0:
                    continue
                term = parts[i] * np.float32(factor)
                total = term if total is None else total + term
            out.append(total)
        return jnp.concatenate(out, axis=0)

    def gradients(field):
        return (
            along_x(field, False),
            jnp.dot(ky[...], field, precision=EXACT, preferred_element_type=F32),
            jnp.dot(field, kzt[...], precision=EXACT, preferred_element_type=F32),
        )

    def operator(field):
        dx, dy, dz = gradients(field)
        return (
            along_x(met[0] * dx, True)
            + jnp.dot(kyt[...], met[1] * dy, precision=EXACT, preferred_element_type=F32)
            + jnp.dot(met[2] * dz, kz[...], precision=EXACT, preferred_element_type=F32)
            + scr[...] * field
        ) * SCALE

    sendv[...] = jnp.zeros_like(sendv)
    work[0] = src[...]
    for c in range(3):
        work[3 + c] = vel[c]
    pl.semaphore_wait(barrier, (GX - 1) + (GY - 1) + (GZ - 1))

    cx = start_x(0, src.at[pl.ds(112, 16)], src.at[pl.ds(0, 16)])
    cv = [
        start_x(3 + c, vel.at[c, pl.ds(112, 16)], vel.at[c, pl.ds(0, 16)]) for c in range(3)
    ]

    owned = (owner[...] == iota((GY, 512), 0)).astype(F32)
    tri = (iota((128, 128), 0) < iota((128, 128), 1)).astype(BF16)
    before = jnp.zeros((GY, 1), F32)
    rank = []
    for b in range(4):
        part = owned[:, 128 * b : 128 * b + 128]
        count = jnp.dot(part.astype(BF16), tri, preferred_element_type=F32) + before
        rank.append(jnp.sum(count * part, axis=0, keepdims=True))
        before = before + jnp.sum(part, axis=1, keepdims=True)
    rank = jnp.concatenate(rank, axis=1)
    slots = (rank.astype(jnp.int32) == iota((CAP, 512), 0)).astype(F32)
    data = jnp.concatenate(
        [coords[...], elem[...].astype(F32), jnp.zeros((4, 512), F32)], axis=0
    )
    lhs = jnp.concatenate([data * owned[g : g + 1, :] for g in range(GY)], axis=0)
    packed = lax.dot_general(
        lhs, slots, (((1,), (1,)), ((), ())), precision=EXACT, preferred_element_type=F32
    )
    for g in range(GY):
        sendp[g] = packed[8 * g : 8 * g + 8, :]

    cy = mid_xy(0, cx)

    to_owner = []
    for k in range(1, GY):
        peer = lax.rem(gy + k, GY)
        to_owner.append(
            remote(sendp.at[peer], recvp.at[gy], pss.at[0, k], prs.at[0, k], (gx, peer, gz))
        )
    recvp[gy] = sendp[gy]

    czp, field = mid_yz(0, cy)
    cvy = []
    for c in range(3):
        cvy.append(mid_xy(3 + c, cv[c]))
    v0 = end_z(0, czp, field)

    cx = start_image(1, operator(v0))
    cvz = []
    vfield = []
    cy = mid_xy(1, cx)
    for c in range(3):
        out, value = mid_yz(3 + c, cvy[c])
        cvz.append(out)
        vfield.append(value)
    cz, field = mid_yz(1, cy)
    for c in range(3):
        value = end_z(3 + c, cvz[c], vfield[c])
        high = value.astype(BF16)
        vhi[pl.ds(128 * c, 128), :] = high
        vlo[pl.ds(128 * c, 128), :] = (value - high.astype(F32)).astype(BF16)
    v1 = end_z(1, cz, field)

    cx = start_image(2, operator(v1))

    for copy in to_owner:
        copy.wait_recv()
    points = gll_points()
    node = iota((8, 128), 0)

    def basis(coord):
        product = lsc[...]
        for m in range(8):
            product = product * jnp.where(node == m, 1.0, coord - np.float32(points[m]))
        return product

    def sample_two(step, carry):
        low_parts, high_parts, weights = [], [], []
        for half in range(2):
            block = recvp[2 * step + half]
            element = block[3:4, :].astype(jnp.int32)
            bx, by, bz = (basis(block[d : d + 1, :]) for d in range(3))
            element_y = element // 16
            element_z = element % 16
            wide = jnp.concatenate(
                [jnp.where(element_z == e, bz, 0.0) for e in range(16)], axis=0
            )
            high = wide.astype(BF16)
            high_parts.append(high)
            low_parts.append((wide - high.astype(F32)).astype(BF16))
            tall = jnp.concatenate(
                [jnp.where(element_y == e, by, 0.0) for e in range(2)], axis=0
            )
            weights.append(
                jnp.concatenate([bx[i : i + 1, :] * tall for i in range(8)], axis=0)
            )
        high = jnp.concatenate(high_parts, axis=1)
        low = jnp.concatenate(low_parts, axis=1)
        for c in range(3):
            vh = vhi[pl.ds(128 * c, 128), :]
            partial = (
                jnp.dot(vh, high, preferred_element_type=F32)
                + jnp.dot(vh, low, preferred_element_type=F32)
                + jnp.dot(vlo[pl.ds(128 * c, 128), :], high, preferred_element_type=F32)
            )
            for half in range(2):
                sendv[2 * step + half, pl.ds(c, 1), :] = jnp.sum(
                    partial[:, 128 * half : 128 * half + 128] * weights[half], axis=0, keepdims=True
                )
        return carry

    lax.fori_loop(0, GY // 2, sample_two, 0)

    cy = mid_xy(2, cx)
    to_home = []
    for k in range(1, GY):
        peer = lax.rem(gy + k, GY)
        to_home.append(
            remote(sendv.at[peer], recvv.at[gy], pss.at[1, k], prs.at[1, k], (gx, peer, gz))
        )
    recvv[gy] = sendv[gy]
    cz, field = mid_yz(2, cy)
    v2 = end_z(2, cz, field)

    place_y = row_id % 16
    share_x = jnp.where((row_id < 16) | (row_id >= 112), 0.5, 1.0)
    edge_y = (place_y % 8 == 0) | (place_y % 8 == 7)
    wall = ((place_y == 0) & at_floor) | ((place_y == 15) & at_ceiling)
    share_y = jnp.where(edge_y & jnp.logical_not(wall), 0.5, 1.0)
    share_z = jnp.where((lane_in == 0) | (lane_in == 7), 0.5, 1.0)
    weight = share_x * share_y * share_z
    dx, dy, dz = gradients(v2)
    products = [
        weight * v0 * v0,
        weight * v0 * v1,
        weight * v1 * v1,
        weight * v1 * v2,
        weight * v2 * v2,
        (met[0] * dx * dx + met[1] * dy * dy + met[2] * dz * dz + scr[...] * v2 * v2) * SCALE,
    ]
    rows = [jnp.sum(value, axis=0, keepdims=True) for value in products]
    rows = jnp.concatenate(rows + [jnp.zeros((2, 128), F32)], axis=0)
    total = jnp.sum(rows, axis=1, keepdims=True)
    row = jnp.sum(
        jnp.where(iota((8, 128), 0) == iota((8, 128), 1), total, 0.0), axis=0, keepdims=True
    )

    def reduce_over(stage, row, count, me, slots_ref, place, base):
        msg[stage] = row
        slots_ref[me] = row
        copies = [
            remote(msg.at[stage], slots_ref.at[me], ass.at[base + k], ars.at[base + k], place(k))
            for k in range(1, count)
        ]
        for copy in copies:
            copy.wait_recv()
        return jnp.sum(slots_ref[...], axis=0)

    row = reduce_over(0, row, GX, gx, rx, at_x, 0)
    row = reduce_over(1, row, GZ, gz, rz, at_z, GX)
    row = reduce_over(2, row, GY, gy, ry, at_y, GX + GZ)

    lane = iota((1, 128), 1)
    m = [jnp.sum(jnp.where(lane == k, row, 0.0), axis=1, keepdims=True) for k in range(6)]

    def form(coefficients, shift):
        total = None
        for i, left in enumerate(coefficients):
            for j, right in enumerate(coefficients):
                term = left * right * m[i + j + shift]
                total = term if total is None else total + term
        return total

    one = jnp.ones_like(m[0])
    rr = m[0]
    direction = [one]
    residual = [one]
    solution_row = [jnp.zeros_like(one)] * 3
    for step in range(3):
        alpha = rr / form(direction, 1)
        for i, value in enumerate(direction):
            solution_row[i] = solution_row[i] + alpha * value
        if step == 2:
            break
        residual = residual + [jnp.zeros_like(one)]
        for i, value in enumerate(direction):
            residual[i + 1] = residual[i + 1] - alpha * value
        new = form(residual, 0)
        beta = new / rr
        direction = [
            value + beta * direction[i] if i < len(direction) else value
            for i, value in enumerate(residual)
        ]
        rr = new
    p_out[...] = (solution_row[0] * v0 + solution_row[1] * v1 + solution_row[2] * v2) * SCALE

    for copy in to_home:
        copy.wait_recv()
    back = jnp.concatenate([recvv[g] for g in range(GY)], axis=0)
    spread = jnp.dot(back, slots, precision=EXACT, preferred_element_type=F32)
    velocity = jnp.zeros((8, 512), F32)
    for g in range(GY):
        velocity = velocity + spread[8 * g : 8 * g + 8, :] * owned[g : g + 1, :]
    pv_out[...] = velocity[0:3, :]

    for copy in sends:
        copy.wait_send()


def body(vel, src, met, scr, coords, owner, elem):
    table = np.array(deriv_table(), np.float32)
    kron = np.kron(np.eye(16, dtype=np.float32), table)
    lsc = np.repeat(np.array(lagrange_scale(), np.float32)[:, None], 128, axis=1)
    operands = (
        vel.reshape(3, 128, 128),
        src.reshape(128, 128),
        met.reshape(3, 128, 128),
        scr.reshape(128, 128),
        coords,
        owner.reshape(1, 512),
        elem.reshape(1, 512),
        jnp.asarray(kron),
        jnp.asarray(kron.T),
        jnp.asarray(kron),
        jnp.asarray(kron.T),
        jnp.asarray(lsc),
    )
    vmem = pl.BlockSpec(memory_space=pltpu.VMEM)
    dma = pltpu.SemaphoreType.DMA
    pressure, velocity = pl.pallas_call(
        kernel,
        out_shape=(
            jax.ShapeDtypeStruct((128, 128), F32),
            jax.ShapeDtypeStruct((3, 512), F32),
        ),
        in_specs=[vmem] * len(operands),
        out_specs=(vmem, vmem),
        scratch_shapes=[
            pltpu.VMEM((FIELDS, 128, 128), F32),
            pltpu.VMEM((2, 2, 16, 128), F32),
            pltpu.VMEM((FIELDS, 2, 16, 128), F32),
            pltpu.VMEM((FIELDS, 2, 8, 128), F32),
            pltpu.VMEM((FIELDS, 2, 8, 128), F32),
            pltpu.VMEM((FIELDS, 2, 1, 128), F32),
            pltpu.VMEM((FIELDS, 2, 1, 128), F32),
            dma((FIELDS, 6)),
            dma((FIELDS, 6)),
            pltpu.VMEM((3, 1, 128), F32),
            pltpu.VMEM((GX, 1, 128), F32),
            pltpu.VMEM((GZ, 1, 128), F32),
            pltpu.VMEM((GY, 1, 128), F32),
            dma((GX + GY + GZ,)),
            dma((GX + GY + GZ,)),
            pltpu.VMEM((GY, 8, 128), F32),
            pltpu.VMEM((GY, 8, 128), F32),
            pltpu.VMEM((GY, 8, 128), F32),
            pltpu.VMEM((GY, 8, 128), F32),
            dma((2, GY)),
            dma((2, GY)),
            pltpu.VMEM((384, 128), BF16),
            pltpu.VMEM((384, 128), BF16),
        ],
        compiler_params=pltpu.CompilerParams(collective_id=0, has_side_effects=True),
        name="step",
    )(*operands)
    return pressure.reshape(8, 16, 128), velocity


def solution(mesh):
    in_specs = (
        P(None, "gx", "gy", "gz"),
        P("gx", "gy", "gz"),
        P(None, "gx", "gy", "gz"),
        P("gx", "gy", "gz"),
        P(None, ("gx", "gy", "gz")),
        P(("gx", "gy", "gz"), None),
        P(("gx", "gy", "gz")),
    )
    out_specs = (P("gx", "gy", "gz"), P(None, ("gx", "gy", "gz")))
    return jax.shard_map(body, mesh=mesh, in_specs=in_specs, out_specs=out_specs, check_vma=False)
```

time: 852 us -> 62.1 us (0.07)
  blocking collectives: 487 us -> 0 us
  local copies, waits for them, and re-layouts: 136 us -> 2.08 us
  other arithmetic: 117 us -> 0 us
  starting transfers between devices: 82.4 us -> 0 us
  Pallas kernels: 0 us -> 59.2 us
  waiting for transfers between devices: 9.64 us -> 0 us
    psum x5 -> x0, blocking collectives: 487 us -> none  [the longest x3 294 us: squares_sum(): return lax.psum(jnp.sum(weight * residual * residual), ('gx', 'gy', 'gz'))]
    while x12 -> x0, other arithmetic: 93 us -> none
    gather x5 -> x0, local copies, waits for them, and re-layouts: 73.4 us -> none  [the longest x4 72.3 us: sample_block(): return sample(element_table[chosen], where_at)]
    ppermute x24 -> x0, starting transfers between devices: 69.7 us -> none  [the longest x12 35.4 us: extended(): lax.ppermute(head, axis, [((i + 1) % count, i) for i in range(count)])]
    pallas_call x0 -> x1, Pallas kernels: none -> 59.2 us  [body(): pl.pallas_call(kernel, out_shape=(jax.ShapeDtypeStruct((128, 128), F32),...]
    while x33 -> x0, local copies, waits for them, and re-layouts: 29.9 us -> none
    all_to_all x2 -> x0, starting transfers between devices: 12.7 us -> none  [the longest x1 6.41 us: body(): lax.all_to_all(values, 'gy', split_axis=1, concat_axis=1, tiled=True)]
    ppermute x24 -> x0, waiting for transfers between devices: 9.63 us -> none  [the longest x12 7.77 us: extended(): lax.ppermute(head, axis, [((i + 1) % count, i) for i in range(count)])]
  transfers between devices with their start and end apart: 26 -> 0, of which waited for: 10 -> 0; matrix products, arithmetic and copies ran while one was open for 28% -> 0% of each run, Pallas kernels for 0% -> 0%
where the time goes in v1:
time: 62.1 us; the launch traced here: 61.9 us
  Pallas kernels  59.2 us (95%)
  local copies, waits for them, and re-layouts  2.08 us (3%)
  between operations  0.65 us (1%)
    pallas_call x1, Pallas kernels, body(): pl.pallas_call(kernel, out_shape=(jax.ShapeDtypeStruct((128, 128), F32),...  59.2 us
    unnamed x4, local copies, waits for them, and re-layouts  2.08 us

profile of v1, /device:TPU:1, one launch (start us, length us, event | category | flops | bytes accessed | tf_op | source)
XLA Modules:
  0.0 61.9 jit_solution(15553785631571565678)
XLA Ops:
  0.6 59.2 %step.1 = (f32[128,128]{1,0:T(8,128)}, f32[3,512]{1,0:T(4,128)}) custom-call(f32[3,128,128]{2,1,0:T(8,128)} %bitcast.7, f32[128,128]{1,0:T(8,128)} %bitcast.9, f32[3,128,128]{2,1,0:T(8,128)} %bitcast.8, f32[128,128]{1,0:T(8,128)} %bitcast.10, f32[3,512]{1,0:T(4,128)} %coords.1, s32[1,512]{1,0:T(1,128)} %bitcast.12, s32[1,512]{1,0:T(1,128)} %bitcast.13, ...), custom_call_target="tpu_custom_call" | custom-call | tf_op jit(solution)/shard_map/step/pallas_call | solution.py:440
  59.8 0.0 copy-start
  59.8 1.5 %copy.15 = f32[8,16,128]{2,1,0:T(8,128)} copy(f32[8,16,128]{2,1,0:T(8,128)} %bitcast.11) | data formatting | bytes 131072
  61.3 0.0 copy-done
  61.3 0.6 copy.16
Async XLA Ops:
  59.8 1.5 %copy-start = (f32[3,512]{1,0:T(4,128)S(1)}, f32[3,512]{1,0:T(4,128)}, u32[]{:S(2)}) copy-start(f32[3,512]{1,0:T(4,128)} %get-tuple-element.9) | copy-start | bytes 18436

commit v2 on v1

--- a/solution.py
+++ b/solution.py
@@ -1,4 +1,4 @@
-import functools
+import itertools
 
 import jax
 import jax.numpy as jnp
@@ -15,7 +15,6 @@
 SCALE = 1.0 / 64.0
 GX, GY, GZ = 4, 16, 8
 CAP = 128
-FIELDS = 6
 
 
 def gll_points():
@@ -70,11 +69,20 @@
     return lax.broadcasted_iota(jnp.int32, shape, dim)
 
 
+DIRECTIONS = sorted(
+    (d for d in itertools.product((-1, 0, 1), repeat=3) if any(d)),
+    key=lambda d: -sum(abs(v) for v in d),
+)
+RING_Y = [k for k in range(2, GY - 1)]
+
+
 def kernel(
-    vel, src, met, scr, coords, owner, elem, ky, kyt, kz, kzt, lsc,
+    vel_in, src_in, met_in, scr_in, coords_in, owner_in, elem_in, ky_in, kyt_in, lsc_in,
     p_out, pv_out,
-    work, hxs, hx, hys, hyr, hzs, hzr, hss, hrs,
-    msg, rx, rz, ry, ass, ars,
+    vel, src, met, scr, coords, owner, elem, ky, kyt, lsc, load_sem,
+    work, hxs, hx, hys, hyr, hes, her, hzs, hzr, hss, hrs,
+    vhx, vys, vyr, vzs, vzr, vss, vrs,
+    msg, rxz, ry, ass, ars,
     sendp, recvp, sendv, recvv, pss, prs, vhi, vlo,
 ):
     gx, gy, gz = lax.axis_index("gx"), lax.axis_index("gy"), lax.axis_index("gz")
@@ -88,13 +96,27 @@
     def at_z(k):
         return (gx, gy, lax.rem(gz + (k + GZ), GZ))
 
+    def near(d):
+        return (
+            lax.rem(gx + (d[0] + GX), GX),
+            lax.rem(gy + (d[1] + GY), GY),
+            lax.rem(gz + (d[2] + GZ), GZ),
+        )
+
     barrier = pltpu.get_barrier_semaphore()
-    for k in range(1, GX):
-        pl.semaphore_signal(barrier, inc=1, device_id=at_x(k), device_id_type=MESH)
-    for k in range(1, GZ):
-        pl.semaphore_signal(barrier, inc=1, device_id=at_z(k), device_id_type=MESH)
-    for k in range(1, GY):
+    for d in DIRECTIONS:
+        pl.semaphore_signal(barrier, inc=1, device_id=near(d), device_id_type=MESH)
+    for k in RING_Y:
         pl.semaphore_signal(barrier, inc=1, device_id=at_y(k), device_id_type=MESH)
+
+    loads = {}
+    for i, (name, source, target) in enumerate((
+        ("src", src_in, src), ("vel", vel_in, vel), ("ky", ky_in, ky), ("kyt", kyt_in, kyt),
+        ("met", met_in, met), ("scr", scr_in, scr), ("coords", coords_in, coords),
+        ("owner", owner_in, owner), ("elem", elem_in, elem), ("lsc", lsc_in, lsc),
+    )):
+        loads[name] = pltpu.make_async_copy(source, target, load_sem.at[i])
+        loads[name].start()
 
     sends = []
 
@@ -120,60 +142,148 @@
     at_floor = gy == 0
     at_ceiling = gy == GY - 1
 
-    def start_x(f, tail, head):
-        return (
-            remote(tail, hx.at[f, 0], hss.at[f, 0], hrs.at[f, 0], at_x(1)),
-            remote(head, hx.at[f, 1], hss.at[f, 1], hrs.at[f, 1], at_x(-1)),
-        )
-
-    def start_image(f, field):
-        work[f] = field
-        hxs[f - 1, 0] = field[112:128, :]
-        hxs[f - 1, 1] = field[0:16, :]
-        return start_x(f, hxs.at[f - 1, 0], hxs.at[f - 1, 1])
-
-    def mid_xy(f, copies):
+    def source_mask():
+        index = iota((16, 128), 0)
+        lane = iota((16, 128), 1)
+        from_x, from_y = index // 3 - 1, index % 3 - 1
+        in_x, in_y = lane // 16, lane % 16
+        keep = (index < 9) & jnp.logical_not((from_y == -1) & at_floor)
+        keep = keep & jnp.logical_not((from_y == 1) & at_ceiling)
+        keep = keep & ((from_x == 0) | ((from_x == -1) & (in_x == 0)) | ((from_x == 1) & (in_x == 7)))
+        return keep & ((from_y == 0) | ((from_y == -1) & (in_y == 0)) | ((from_y == 1) & (in_y == 15)))
+
+    z_keep = source_mask()
+
+    def start_halo(f, field):
         w = work.at[f]
-        copies[0].wait_recv()
-        w[pl.ds(0, 16), :] = w[pl.ds(0, 16), :] + hx[f, 0]
-        copies[1].wait_recv()
-        w[pl.ds(112, 16), :] = w[pl.ds(112, 16), :] + hx[f, 1]
+        w[...] = field
         both = w[pl.ds(7, 8, stride=16), :] + w[pl.ds(8, 8, stride=16), :]
         w[pl.ds(7, 8, stride=16), :] = both
         w[pl.ds(8, 8, stride=16), :] = both
-        hys[f, 0] = w[pl.ds(15, 8, stride=16), :]
-        hys[f, 1] = w[pl.ds(0, 8, stride=16), :]
-        return (
-            remote(hys.at[f, 0], hyr.at[f, 0], hss.at[f, 2], hrs.at[f, 2], at_y(1)),
-            remote(hys.at[f, 1], hyr.at[f, 1], hss.at[f, 3], hrs.at[f, 3], at_y(-1)),
-        )
-
-    def mid_yz(f, copies):
-        w = work.at[f]
-        copies[0].wait_recv()
-        w[pl.ds(0, 8, stride=16), :] = w[pl.ds(0, 8, stride=16), :] + jnp.where(at_floor, 0.0, hyr[f, 0])
-        copies[1].wait_recv()
-        w[pl.ds(15, 8, stride=16), :] = w[pl.ds(15, 8, stride=16), :] + jnp.where(at_ceiling, 0.0, hyr[f, 1])
         field = w[...]
-        hzs[f, 0] = jnp.sum(jnp.where(eye, field[:, 127:128], 0.0), axis=0, keepdims=True)
-        hzs[f, 1] = jnp.sum(jnp.where(eye, field[:, 0:1], 0.0), axis=0, keepdims=True)
-        out = (
-            remote(hzs.at[f, 0], hzr.at[f, 0], hss.at[f, 4], hrs.at[f, 4], at_z(1)),
-            remote(hzs.at[f, 1], hzr.at[f, 1], hss.at[f, 5], hrs.at[f, 5], at_z(-1)),
-        )
+        pair = jnp.concatenate(
+            [
+                jnp.sum(jnp.where(eye, field[:, 127:128], 0.0), axis=0, keepdims=True),
+                jnp.sum(jnp.where(eye, field[:, 0:1], 0.0), axis=0, keepdims=True),
+            ],
+            axis=0,
+        )
+        for dx in (-1, 0, 1):
+            for dy in (-1, 0, 1):
+                shift = (16 * dx - 15 * dy) % 128
+                hzs[f, (1 - dx) * 3 + (1 - dy)] = pltpu.roll(pair, shift, 1) if shift else pair
+        copies = {}
+
+        def send(d, source, target):
+            k = DIRECTIONS.index(d)
+            copies[d] = remote(source, target, hss.at[f, k], hrs.at[f, k], near(d))
+
+        for d in DIRECTIONS:
+            if d[2]:
+                j, side = (1 - d[0]) * 3 + (1 - d[1]), (1 - d[2]) // 2
+                send(d, hzs.at[f, j, pl.ds(side, 1)], hzr.at[f, side, pl.ds(j, 1)])
         field = (
             field
             + jnp.where(low_z, pltpu.roll(field, 1, 1), 0.0)
             + jnp.where(high_z, pltpu.roll(field, 127, 1), 0.0)
         )
-        return out, field
-
-    def end_z(f, copies, field):
+        w[...] = field
+        for d in DIRECTIONS:
+            if d[2] == 0 and d[0] and d[1]:
+                e = (1 - d[0]) + (1 - d[1]) // 2
+                row = (112 if d[0] == 1 else 0) + (15 if d[1] == 1 else 0)
+                hes[f, e] = field[row : row + 1, :]
+                send(d, hes.at[f, e], her.at[f, e])
+        hxs[f, 0] = field[112:128, :]
+        hxs[f, 1] = field[0:16, :]
+        send((1, 0, 0), hxs.at[f, 0], hx.at[f, 0])
+        send((-1, 0, 0), hxs.at[f, 1], hx.at[f, 1])
+        hys[f, 0] = w[pl.ds(15, 8, stride=16), :]
+        hys[f, 1] = w[pl.ds(0, 8, stride=16), :]
+        send((0, 1, 0), hys.at[f, 0], hyr.at[f, 0])
+        send((0, -1, 0), hys.at[f, 1], hyr.at[f, 1])
+        return copies
+
+    def end_halo(f, copies):
+        w = work.at[f]
+        copies[0, 1, 0].wait_recv()
+        w[pl.ds(0, 8, stride=16), :] = w[pl.ds(0, 8, stride=16), :] + jnp.where(at_floor, 0.0, hyr[f, 0])
+        copies[0, -1, 0].wait_recv()
+        w[pl.ds(15, 8, stride=16), :] = w[pl.ds(15, 8, stride=16), :] + jnp.where(at_ceiling, 0.0, hyr[f, 1])
+        copies[1, 0, 0].wait_recv()
+        w[pl.ds(0, 16), :] = w[pl.ds(0, 16), :] + hx[f, 0]
+        copies[-1, 0, 0].wait_recv()
+        w[pl.ds(112, 16), :] = w[pl.ds(112, 16), :] + hx[f, 1]
+        for d in DIRECTIONS:
+            if d[2] == 0 and d[0] and d[1]:
+                e = (1 - d[0]) + (1 - d[1]) // 2
+                row = (0 if d[0] == 1 else 112) + (0 if d[1] == 1 else 15)
+                copies[d].wait_recv()
+                cut = at_floor if d[1] == 1 else at_ceiling
+                w[pl.ds(row, 1), :] = w[pl.ds(row, 1), :] + jnp.where(cut, 0.0, her[f, e])
+        field = w[...]
+        for d in reversed(DIRECTIONS):
+            if d[2]:
+                copies[d].wait_recv()
+        low = jnp.sum(jnp.where(z_keep, hzr[f, 0], 0.0), axis=0, keepdims=True)
+        high = jnp.sum(jnp.where(z_keep, hzr[f, 1], 0.0), axis=0, keepdims=True)
+        low = jnp.sum(jnp.where(eye, low, 0.0), axis=1, keepdims=True)
+        high = jnp.sum(jnp.where(eye, high, 0.0), axis=1, keepdims=True)
+        return field + jnp.where(lane_id == 0, low, 0.0) + jnp.where(lane_id == 127, high, 0.0)
+
+    def start_x(c):
+        return (
+            remote(vel.at[c, pl.ds(112, 16)], vhx.at[c, 0], vss.at[c, 0], vrs.at[c, 0], at_x(1)),
+            remote(vel.at[c, pl.ds(0, 16)], vhx.at[c, 1], vss.at[c, 1], vrs.at[c, 1], at_x(-1)),
+        )
+
+    def mid_xy(c, copies):
+        w = work.at[3 + c]
+        w[...] = vel[c]
         copies[0].wait_recv()
-        low = jnp.sum(jnp.where(eye, hzr[f, 0], 0.0), axis=1, keepdims=True)
+        w[pl.ds(0, 16), :] = w[pl.ds(0, 16), :] + vhx[c, 0]
         copies[1].wait_recv()
-        high = jnp.sum(jnp.where(eye, hzr[f, 1], 0.0), axis=1, keepdims=True)
-        return field + jnp.where(lane_id == 0, low, 0.0) + jnp.where(lane_id == 127, high, 0.0)
+        w[pl.ds(112, 16), :] = w[pl.ds(112, 16), :] + vhx[c, 1]
+        both = w[pl.ds(7, 8, stride=16), :] + w[pl.ds(8, 8, stride=16), :]
+        w[pl.ds(7, 8, stride=16), :] = both
+        w[pl.ds(8, 8, stride=16), :] = both
+        vys[c, 0] = w[pl.ds(15, 8, stride=16), :]
+        vys[c, 1] = w[pl.ds(0, 8, stride=16), :]
+        return (
+            remote(vys.at[c, 0], vyr.at[c, 0], vss.at[c, 2], vrs.at[c, 2], at_y(1)),
+            remote(vys.at[c, 1], vyr.at[c, 1], vss.at[c, 3], vrs.at[c, 3], at_y(-1)),
+        )
+
+    def mid_yz(c, copies):
+        w = work.at[3 + c]
+        copies[0].wait_recv()
+        w[pl.ds(0, 8, stride=16), :] = w[pl.ds(0, 8, stride=16), :] + jnp.where(at_floor, 0.0, vyr[c, 0])
+        copies[1].wait_recv()
+        w[pl.ds(15, 8, stride=16), :] = w[pl.ds(15, 8, stride=16), :] + jnp.where(at_ceiling, 0.0, vyr[c, 1])
+        field = w[...]
+        vzs[c, 0] = jnp.sum(jnp.where(eye, field[:, 127:128], 0.0), axis=0, keepdims=True)
+        vzs[c, 1] = jnp.sum(jnp.where(eye, field[:, 0:1], 0.0), axis=0, keepdims=True)
+        out = (
+            remote(vzs.at[c, 0], vzr.at[c, 0], vss.at[c, 4], vrs.at[c, 4], at_z(1)),
+            remote(vzs.at[c, 1], vzr.at[c, 1], vss.at[c, 5], vrs.at[c, 5], at_z(-1)),
+        )
+        w[...] = (
+            field
+            + jnp.where(low_z, pltpu.roll(field, 1, 1), 0.0)
+            + jnp.where(high_z, pltpu.roll(field, 127, 1), 0.0)
+        )
+        return out
+
+    def end_z(c, copies):
+        field = work[3 + c]
+        copies[0].wait_recv()
+        low = jnp.sum(jnp.where(eye, vzr[c, 0], 0.0), axis=1, keepdims=True)
+        copies[1].wait_recv()
+        high = jnp.sum(jnp.where(eye, vzr[c, 1], 0.0), axis=1, keepdims=True)
+        field = field + jnp.where(lane_id == 0, low, 0.0) + jnp.where(lane_id == 127, high, 0.0)
+        high = field.astype(BF16)
+        vhi[pl.ds(128 * c, 128), :] = high
+        vlo[pl.ds(128 * c, 128), :] = (field - high.astype(F32)).astype(BF16)
 
     table = deriv_table()
 
@@ -195,7 +305,7 @@
         return (
             along_x(field, False),
             jnp.dot(ky[...], field, precision=EXACT, preferred_element_type=F32),
-            jnp.dot(field, kzt[...], precision=EXACT, preferred_element_type=F32),
+            jnp.dot(field, kyt[...], precision=EXACT, preferred_element_type=F32),
         )
 
     def operator(field):
@@ -203,21 +313,20 @@
         return (
             along_x(met[0] * dx, True)
             + jnp.dot(kyt[...], met[1] * dy, precision=EXACT, preferred_element_type=F32)
-            + jnp.dot(met[2] * dz, kz[...], precision=EXACT, preferred_element_type=F32)
+            + jnp.dot(met[2] * dz, ky[...], precision=EXACT, preferred_element_type=F32)
             + scr[...] * field
         ) * SCALE
 
     sendv[...] = jnp.zeros_like(sendv)
-    work[0] = src[...]
-    for c in range(3):
-        work[3 + c] = vel[c]
-    pl.semaphore_wait(barrier, (GX - 1) + (GY - 1) + (GZ - 1))
-
-    cx = start_x(0, src.at[pl.ds(112, 16)], src.at[pl.ds(0, 16)])
-    cv = [
-        start_x(3 + c, vel.at[c, pl.ds(112, 16)], vel.at[c, pl.ds(0, 16)]) for c in range(3)
-    ]
-
+    loads["src"].wait()
+    pl.semaphore_wait(barrier, len(DIRECTIONS) + len(RING_Y))
+    halo = start_halo(0, src[...])
+    loads["vel"].wait()
+    cvx = [start_x(c) for c in range(3)]
+
+    loads["coords"].wait()
+    loads["owner"].wait()
+    loads["elem"].wait()
     owned = (owner[...] == iota((GY, 512), 0)).astype(F32)
     tri = (iota((128, 128), 0) < iota((128, 128), 1)).astype(BF16)
     before = jnp.zeros((GY, 1), F32)
@@ -239,8 +348,6 @@
     for g in range(GY):
         sendp[g] = packed[8 * g : 8 * g + 8, :]
 
-    cy = mid_xy(0, cx)
-
     to_owner = []
     for k in range(1, GY):
         peer = lax.rem(gy + k, GY)
@@ -249,30 +356,21 @@
         )
     recvp[gy] = sendp[gy]
 
-    czp, field = mid_yz(0, cy)
-    cvy = []
+    cvy = [mid_xy(c, cvx[c]) for c in range(3)]
+    loads["ky"].wait()
+    loads["kyt"].wait()
+    loads["met"].wait()
+    loads["scr"].wait()
+    v0 = end_halo(0, halo)
+
+    halo = start_halo(1, operator(v0))
+    cvz = [mid_yz(c, cvy[c]) for c in range(3)]
+    v1 = end_halo(1, halo)
+    halo = start_halo(2, operator(v1))
     for c in range(3):
-        cvy.append(mid_xy(3 + c, cv[c]))
-    v0 = end_z(0, czp, field)
-
-    cx = start_image(1, operator(v0))
-    cvz = []
-    vfield = []
-    cy = mid_xy(1, cx)
-    for c in range(3):
-        out, value = mid_yz(3 + c, cvy[c])
-        cvz.append(out)
-        vfield.append(value)
-    cz, field = mid_yz(1, cy)
-    for c in range(3):
-        value = end_z(3 + c, cvz[c], vfield[c])
-        high = value.astype(BF16)
-        vhi[pl.ds(128 * c, 128), :] = high
-        vlo[pl.ds(128 * c, 128), :] = (value - high.astype(F32)).astype(BF16)
-    v1 = end_z(1, cz, field)
-
-    cx = start_image(2, operator(v1))
-
+        end_z(c, cvz[c])
+
+    loads["lsc"].wait()
     for copy in to_owner:
         copy.wait_recv()
     points = gll_points()
@@ -321,7 +419,6 @@
 
     lax.fori_loop(0, GY // 2, sample_two, 0)
 
-    cy = mid_xy(2, cx)
     to_home = []
     for k in range(1, GY):
         peer = lax.rem(gy + k, GY)
@@ -329,8 +426,7 @@
             remote(sendv.at[peer], recvv.at[gy], pss.at[1, k], prs.at[1, k], (gx, peer, gz))
         )
     recvv[gy] = sendv[gy]
-    cz, field = mid_yz(2, cy)
-    v2 = end_z(2, cz, field)
+    v2 = end_halo(2, halo)
 
     place_y = row_id % 16
     share_x = jnp.where((row_id < 16) | (row_id >= 112), 0.5, 1.0)
@@ -355,20 +451,38 @@
         jnp.where(iota((8, 128), 0) == iota((8, 128), 1), total, 0.0), axis=0, keepdims=True
     )
 
-    def reduce_over(stage, row, count, me, slots_ref, place, base):
-        msg[stage] = row
-        slots_ref[me] = row
-        copies = [
-            remote(msg.at[stage], slots_ref.at[me], ass.at[base + k], ars.at[base + k], place(k))
-            for k in range(1, count)
-        ]
-        for copy in copies:
-            copy.wait_recv()
-        return jnp.sum(slots_ref[...], axis=0)
-
-    row = reduce_over(0, row, GX, gx, rx, at_x, 0)
-    row = reduce_over(1, row, GZ, gz, rz, at_z, GX)
-    row = reduce_over(2, row, GY, gy, ry, at_y, GX + GZ)
+    msg[0] = row
+    here = gx * GZ + gz
+    rxz[here] = row
+    copies = []
+    for i in range(GX):
+        for k in range(GZ):
+            if i or k:
+                n = i * GZ + k
+                device = (lax.rem(gx + i, GX), gy, lax.rem(gz + k, GZ))
+                copies.append(remote(msg.at[0], rxz.at[here], ass.at[n], ars.at[n], device))
+    for copy in copies:
+        copy.wait_recv()
+    row = jnp.sum(rxz[...], axis=0)
+    msg[1] = row
+    ry[gy] = row
+    copies = []
+    for k in range(1, GY):
+        n = GX * GZ + k
+        copies.append(remote(msg.at[1], ry.at[gy], ass.at[n], ars.at[n], at_y(k)))
+
+    for copy in to_home:
+        copy.wait_recv()
+    back = jnp.concatenate([recvv[g] for g in range(GY)], axis=0)
+    spread = jnp.dot(back, slots, precision=EXACT, preferred_element_type=F32)
+    velocity = jnp.zeros((8, 512), F32)
+    for g in range(GY):
+        velocity = velocity + spread[8 * g : 8 * g + 8, :] * owned[g : g + 1, :]
+    pv_out[...] = velocity[0:3, :]
+
+    for copy in copies:
+        copy.wait_recv()
+    row = jnp.sum(ry[...], axis=0)
 
     lane = iota((1, 128), 1)
     m = [jnp.sum(jnp.where(lane == k, row, 0.0), axis=1, keepdims=True) for k in range(6)]
@@ -404,15 +518,6 @@
         rr = new
     p_out[...] = (solution_row[0] * v0 + solution_row[1] * v1 + solution_row[2] * v2) * SCALE
 
-    for copy in to_home:
-        copy.wait_recv()
-    back = jnp.concatenate([recvv[g] for g in range(GY)], axis=0)
-    spread = jnp.dot(back, slots, precision=EXACT, preferred_element_type=F32)
-    velocity = jnp.zeros((8, 512), F32)
-    for g in range(GY):
-        velocity = velocity + spread[8 * g : 8 * g + 8, :] * owned[g : g + 1, :]
-    pv_out[...] = velocity[0:3, :]
-
     for copy in sends:
         copy.wait_send()
 
@@ -431,10 +536,9 @@
         elem.reshape(1, 512),
         jnp.asarray(kron),
         jnp.asarray(kron.T),
-        jnp.asarray(kron),
-        jnp.asarray(kron.T),
         jnp.asarray(lsc),
     )
+    anywhere = pl.BlockSpec(memory_space=pl.ANY)
     vmem = pl.BlockSpec(memory_space=pltpu.VMEM)
     dma = pltpu.SemaphoreType.DMA
     pressure, velocity = pl.pallas_call(
@@ -443,24 +547,34 @@
             jax.ShapeDtypeStruct((128, 128), F32),
             jax.ShapeDtypeStruct((3, 512), F32),
         ),
-        in_specs=[vmem] * len(operands),
+        in_specs=[anywhere] * len(operands),
         out_specs=(vmem, vmem),
-        scratch_shapes=[
-            pltpu.VMEM((FIELDS, 128, 128), F32),
-            pltpu.VMEM((2, 2, 16, 128), F32),
-            pltpu.VMEM((FIELDS, 2, 16, 128), F32),
-            pltpu.VMEM((FIELDS, 2, 8, 128), F32),
-            pltpu.VMEM((FIELDS, 2, 8, 128), F32),
-            pltpu.VMEM((FIELDS, 2, 1, 128), F32),
-            pltpu.VMEM((FIELDS, 2, 1, 128), F32),
-            dma((FIELDS, 6)),
-            dma((FIELDS, 6)),
-            pltpu.VMEM((3, 1, 128), F32),
-            pltpu.VMEM((GX, 1, 128), F32),
-            pltpu.VMEM((GZ, 1, 128), F32),
+        scratch_shapes=[pltpu.VMEM(x.shape, x.dtype) for x in operands]
+        + [
+            dma((len(operands),)),
+            pltpu.VMEM((6, 128, 128), F32),
+            pltpu.VMEM((3, 2, 16, 128), F32),
+            pltpu.VMEM((3, 2, 16, 128), F32),
+            pltpu.VMEM((3, 2, 8, 128), F32),
+            pltpu.VMEM((3, 2, 8, 128), F32),
+            pltpu.VMEM((3, 4, 1, 128), F32),
+            pltpu.VMEM((3, 4, 1, 128), F32),
+            pltpu.VMEM((3, 9, 2, 128), F32),
+            pltpu.VMEM((3, 2, 16, 128), F32),
+            dma((3, 26)),
+            dma((3, 26)),
+            pltpu.VMEM((3, 2, 16, 128), F32),
+            pltpu.VMEM((3, 2, 8, 128), F32),
+            pltpu.VMEM((3, 2, 8, 128), F32),
+            pltpu.VMEM((3, 2, 1, 128), F32),
+            pltpu.VMEM((3, 2, 1, 128), F32),
+            dma((3, 6)),
+            dma((3, 6)),
+            pltpu.VMEM((2, 1, 128), F32),
+            pltpu.VMEM((GX * GZ, 1, 128), F32),
             pltpu.VMEM((GY, 1, 128), F32),
-            dma((GX + GY + GZ,)),
-            dma((GX + GY + GZ,)),
+            dma((GX * GZ + GY,)),
+            dma((GX * GZ + GY,)),
             pltpu.VMEM((GY, 8, 128), F32),
             pltpu.VMEM((GY, 8, 128), F32),
             pltpu.VMEM((GY, 8, 128), F32),

time: 62.1 us -> 49.7 us (0.80)
  Pallas kernels: 59.2 us -> 46.8 us
    pallas_call x1, Pallas kernels: 59.2 us -> 46.8 us  [body(): pl.pallas_call(kernel, out_shape=(jax.ShapeDtypeStruct((128, 128), F32),...]
where the time goes in v2:
time: 49.7 us; the launch traced here: 49.5 us
  Pallas kernels  46.8 us (94%)
  local copies, waits for them, and re-layouts  2.08 us (4%)
  between operations  0.65 us (1%)
    pallas_call x1, Pallas kernels, body(): pl.pallas_call(kernel, out_shape=(jax.ShapeDtypeStruct((128, 128), F32),...  46.8 us
    unnamed x4, local copies, waits for them, and re-layouts  2.08 us

profile of v2, /device:TPU:1, one launch (start us, length us, event | category | flops | bytes accessed | tf_op | source)
XLA Modules:
  0.0 49.5 jit_solution(10749864068035022028)
XLA Ops:
  0.6 46.8 %step.1 = (f32[128,128]{1,0:T(8,128)}, f32[3,512]{1,0:T(4,128)}) custom-call(f32[3,128,128]{2,1,0:T(8,128)} %bitcast.7, f32[128,128]{1,0:T(8,128)} %bitcast.10, f32[3,128,128]{2,1,0:T(8,128)} %bitcast.8, f32[128,128]{1,0:T(8,128)} %bitcast.11, f32[3,512]{1,0:T(4,128)} %coords_in.1, s32[1,512]{1,0:T(1,128)} %bitcast.12, s32[1,512]{1,0:T(1,128)} %bitcast.13, ...), custom_call_target="tpu_custom_call" | custom-call | tf_op jit(solution)/shard_map/step/pallas_call | solution.py:544
  47.4 0.0 copy-start
  47.4 1.5 %copy.14 = f32[8,16,128]{2,1,0:T(8,128)} copy(f32[8,16,128]{2,1,0:T(8,128)} %bitcast.9) | data formatting | bytes 131072
  48.9 0.0 copy-done
  48.9 0.6 %copy.15 = f32[3,512]{1,0:T(4,128)} copy(f32[3,512]{1,0:T(4,128)S(1)} %copy-done) | data formatting | bytes 12288
Async XLA Ops:
  47.4 1.5 %copy-start = (f32[3,512]{1,0:T(4,128)S(1)}, f32[3,512]{1,0:T(4,128)}, u32[]{:S(2)}) copy-start(f32[3,512]{1,0:T(4,128)} %get-tuple-element.9) | copy-start | bytes 18436

commit v3 on v2

--- a/solution.py
+++ b/solution.py
@@ -154,7 +154,7 @@
 
     z_keep = source_mask()
 
-    def start_halo(f, field):
+    def pack_planes(f, field):
         w = work.at[f]
         w[...] = field
         both = w[pl.ds(7, 8, stride=16), :] + w[pl.ds(8, 8, stride=16), :]
@@ -172,16 +172,10 @@
             for dy in (-1, 0, 1):
                 shift = (16 * dx - 15 * dy) % 128
                 hzs[f, (1 - dx) * 3 + (1 - dy)] = pltpu.roll(pair, shift, 1) if shift else pair
-        copies = {}
-
-        def send(d, source, target):
-            k = DIRECTIONS.index(d)
-            copies[d] = remote(source, target, hss.at[f, k], hrs.at[f, k], near(d))
-
-        for d in DIRECTIONS:
-            if d[2]:
-                j, side = (1 - d[0]) * 3 + (1 - d[1]), (1 - d[2]) // 2
-                send(d, hzs.at[f, j, pl.ds(side, 1)], hzr.at[f, side, pl.ds(j, 1)])
+        return field
+
+    def pack_faces(f, field):
+        w = work.at[f]
         field = (
             field
             + jnp.where(low_z, pltpu.roll(field, 1, 1), 0.0)
@@ -190,18 +184,36 @@
         w[...] = field
         for d in DIRECTIONS:
             if d[2] == 0 and d[0] and d[1]:
-                e = (1 - d[0]) + (1 - d[1]) // 2
                 row = (112 if d[0] == 1 else 0) + (15 if d[1] == 1 else 0)
-                hes[f, e] = field[row : row + 1, :]
-                send(d, hes.at[f, e], her.at[f, e])
+                hes[f, (1 - d[0]) + (1 - d[1]) // 2] = field[row : row + 1, :]
         hxs[f, 0] = field[112:128, :]
         hxs[f, 1] = field[0:16, :]
-        send((1, 0, 0), hxs.at[f, 0], hx.at[f, 0])
-        send((-1, 0, 0), hxs.at[f, 1], hx.at[f, 1])
         hys[f, 0] = w[pl.ds(15, 8, stride=16), :]
         hys[f, 1] = w[pl.ds(0, 8, stride=16), :]
-        send((0, 1, 0), hys.at[f, 0], hyr.at[f, 0])
-        send((0, -1, 0), hys.at[f, 1], hyr.at[f, 1])
+
+    def send_halo(f, copies, planes):
+        for d in DIRECTIONS:
+            if planes != (d[2] != 0):
+                continue
+            k = DIRECTIONS.index(d)
+            if d[2]:
+                j, side = (1 - d[0]) * 3 + (1 - d[1]), (1 - d[2]) // 2
+                source, target = hzs.at[f, j, pl.ds(side, 1)], hzr.at[f, side, pl.ds(j, 1)]
+            elif d[0] and d[1]:
+                e = (1 - d[0]) + (1 - d[1]) // 2
+                source, target = hes.at[f, e], her.at[f, e]
+            elif d[0]:
+                source, target = hxs.at[f, (1 - d[0]) // 2], hx.at[f, (1 - d[0]) // 2]
+            else:
+                source, target = hys.at[f, (1 - d[1]) // 2], hyr.at[f, (1 - d[1]) // 2]
+            copies[d] = remote(source, target, hss.at[f, k], hrs.at[f, k], near(d))
+
+    def start_halo(f, field):
+        copies = {}
+        field = pack_planes(f, field)
+        send_halo(f, copies, True)
+        pack_faces(f, field)
+        send_halo(f, copies, False)
         return copies
 
     def end_halo(f, copies):
@@ -319,8 +331,11 @@
 
     sendv[...] = jnp.zeros_like(sendv)
     loads["src"].wait()
+    pack_faces(0, pack_planes(0, src[...]))
     pl.semaphore_wait(barrier, len(DIRECTIONS) + len(RING_Y))
-    halo = start_halo(0, src[...])
+    halo = {}
+    send_halo(0, halo, True)
+    send_halo(0, halo, False)
     loads["vel"].wait()
     cvx = [start_x(c) for c in range(3)]
 
@@ -363,10 +378,26 @@
     loads["scr"].wait()
     v0 = end_halo(0, halo)
 
-    halo = start_halo(1, operator(v0))
+    image0 = operator(v0)
+    halo = start_halo(1, image0)
     cvz = [mid_yz(c, cvy[c]) for c in range(3)]
     v1 = end_halo(1, halo)
-    halo = start_halo(2, operator(v1))
+    image1 = operator(v1)
+    halo = start_halo(2, image1)
+    place_y = row_id % 16
+    share_x = jnp.where((row_id < 16) | (row_id >= 112), 0.5, 1.0)
+    edge_y = (place_y % 8 == 0) | (place_y % 8 == 7)
+    wall = ((place_y == 0) & at_floor) | ((place_y == 15) & at_ceiling)
+    share_y = jnp.where(edge_y & jnp.logical_not(wall), 0.5, 1.0)
+    share_z = jnp.where((lane_in == 0) | (lane_in == 7), 0.5, 1.0)
+    weight = share_x * share_y * share_z
+    early = jnp.concatenate(
+        [
+            jnp.sum(value, axis=0, keepdims=True)
+            for value in (weight * v0 * v0, v0 * image0, weight * v1 * v1, v1 * image1)
+        ],
+        axis=0,
+    )
     for c in range(3):
         end_z(c, cvz[c])
 
@@ -428,24 +459,20 @@
     recvv[gy] = sendv[gy]
     v2 = end_halo(2, halo)
 
-    place_y = row_id % 16
-    share_x = jnp.where((row_id < 16) | (row_id >= 112), 0.5, 1.0)
-    edge_y = (place_y % 8 == 0) | (place_y % 8 == 7)
-    wall = ((place_y == 0) & at_floor) | ((place_y == 15) & at_ceiling)
-    share_y = jnp.where(edge_y & jnp.logical_not(wall), 0.5, 1.0)
-    share_z = jnp.where((lane_in == 0) | (lane_in == 7), 0.5, 1.0)
-    weight = share_x * share_y * share_z
     dx, dy, dz = gradients(v2)
-    products = [
-        weight * v0 * v0,
-        weight * v0 * v1,
-        weight * v1 * v1,
-        weight * v1 * v2,
-        weight * v2 * v2,
-        (met[0] * dx * dx + met[1] * dy * dy + met[2] * dz * dz + scr[...] * v2 * v2) * SCALE,
-    ]
-    rows = [jnp.sum(value, axis=0, keepdims=True) for value in products]
-    rows = jnp.concatenate(rows + [jnp.zeros((2, 128), F32)], axis=0)
+    rows = jnp.concatenate(
+        [
+            early,
+            jnp.sum(weight * v2 * v2, axis=0, keepdims=True),
+            jnp.sum(
+                (met[0] * dx * dx + met[1] * dy * dy + met[2] * dz * dz + scr[...] * v2 * v2) * SCALE,
+                axis=0,
+                keepdims=True,
+            ),
+            jnp.zeros((2, 128), F32),
+        ],
+        axis=0,
+    )
     total = jnp.sum(rows, axis=1, keepdims=True)
     row = jnp.sum(
         jnp.where(iota((8, 128), 0) == iota((8, 128), 1), total, 0.0), axis=0, keepdims=True
@@ -544,8 +571,8 @@
     pressure, velocity = pl.pallas_call(
         kernel,
         out_shape=(
-            jax.ShapeDtypeStruct((128, 128), F32),
-            jax.ShapeDtypeStruct((3, 512), F32),
+            pltpu.VMEM((128, 128), F32),
+            pltpu.VMEM((3, 512), F32),
         ),
         in_specs=[anywhere] * len(operands),
         out_specs=(vmem, vmem),

time: 49.7 us -> 47.9 us (0.964)
  Pallas kernels: 46.8 us -> 45.9 us
  local copies, waits for them, and re-layouts: 2.08 us -> 1.23 us
    pallas_call x1, Pallas kernels: 46.8 us -> 45.9 us  [body(): pl.pallas_call(kernel, out_shape=(pltpu.VMEM((128, 128), F32), pltpu.VMEM...]
    unnamed x4 -> x2, local copies, waits for them, and re-layouts: 2.08 us -> 1.23 us
where the time goes in v3:
time: 47.9 us; the launch traced here: 47.8 us
  Pallas kernels  45.9 us (96%)
  local copies, waits for them, and re-layouts  1.23 us (3%)
  between operations  0.64 us (1%)
    pallas_call x1, Pallas kernels, body(): pl.pallas_call(kernel, out_shape=(pltpu.VMEM((128, 128), F32), pltpu.VMEM...  45.9 us
    unnamed x2, local copies, waits for them, and re-layouts  1.23 us

profile of v3, /device:TPU:1, one launch (start us, length us, event | category | flops | bytes accessed | tf_op | source)
XLA Modules:
  0.0 47.8 jit_solution(14772736594125427163)
XLA Ops:
  0.6 45.9 %step.1 = (f32[128,128]{1,0:T(8,128)S(1)}, f32[3,512]{1,0:T(4,128)S(1)}) custom-call(f32[3,128,128]{2,1,0:T(8,128)} %bitcast.8, f32[128,128]{1,0:T(8,128)} %bitcast.10, f32[3,128,128]{2,1,0:T(8,128)} %bitcast.9, f32[128,128]{1,0:T(8,128)} %bitcast.11, f32[3,512]{1,0:T(4,128)} %coords_in.1, s32[1,512]{1,0:T(1,128)} %bitcast.12, s32[1,512]{1,0:T(1,128)} %bitcast.13, ...), custom_call_target="tpu_custom_call" | custom-call | tf_op jit(solution)/shard_map/step/pallas_call | solution.py:571
  46.5 0.6 %copy.14 = f32[8,16,128]{2,1,0:T(8,128)} copy(f32[8,16,128]{2,1,0:T(8,128)S(1)} %bitcast.7) | data formatting | bytes 131072
  47.2 0.6 %copy.15 = f32[3,512]{1,0:T(4,128)} copy(f32[3,512]{1,0:T(4,128)S(1)} %get-tuple-element.7) | data formatting | bytes 12288

commit v4 on v3

--- a/solution.py
+++ b/solution.py
@@ -73,6 +73,7 @@
     (d for d in itertools.product((-1, 0, 1), repeat=3) if any(d)),
     key=lambda d: -sum(abs(v) for v in d),
 )
+SENT_ROWS = 3 * 70 + 150 + 31 + 15 + 2 * 120
 RING_Y = [k for k in range(2, GY - 1)]
 
 
@@ -80,10 +81,11 @@
     vel_in, src_in, met_in, scr_in, coords_in, owner_in, elem_in, ky_in, kyt_in, lsc_in,
     p_out, pv_out,
     vel, src, met, scr, coords, owner, elem, ky, kyt, lsc, load_sem,
-    work, hxs, hx, hys, hyr, hes, her, hzs, hzr, hss, hrs,
-    vhx, vys, vyr, vzs, vzr, vss, vrs,
-    msg, rxz, ry, ass, ars,
-    sendp, recvp, sendv, recvv, pss, prs, vhi, vlo,
+    work, hxs, hx, hys, hyr, hes, her, hzs, hzr, halo_sem,
+    vhx, vys, vyr, vzs, vzr, velocity_sem,
+    msg, rxz, ry, sum_sem,
+    sendp, recvp, sendv, recvv, particle_sem, vhi, vlo,
+    send_sem, measure,
 ):
     gx, gy, gz = lax.axis_index("gx"), lax.axis_index("gy"), lax.axis_index("gz")
 
@@ -118,20 +120,22 @@
         loads[name] = pltpu.make_async_copy(source, target, load_sem.at[i])
         loads[name].start()
 
-    sends = []
-
-    def remote(src_ref, dst_ref, ssem, rsem, device):
-        copy = pltpu.make_async_remote_copy(
-            src_ref=src_ref,
-            dst_ref=dst_ref,
-            send_sem=ssem,
-            recv_sem=rsem,
+    sent_rows = []
+
+    def remote(source, target, sem, device, rows):
+        pltpu.make_async_remote_copy(
+            src_ref=source,
+            dst_ref=target,
+            send_sem=send_sem.at[0],
+            recv_sem=sem,
             device_id=device,
             device_id_type=MESH,
-        )
-        copy.start()
-        sends.append(copy)
-        return copy
+        ).start()
+        sent_rows.append(rows)
+
+    def wait_rows(sem, rows):
+        piece = measure.at[pl.ds(0, rows)]
+        pltpu.make_async_copy(piece, piece, sem).wait()
 
     row_id = iota((128, 128), 0)
     lane_id = iota((128, 128), 1)
@@ -191,11 +195,11 @@
         hys[f, 0] = w[pl.ds(15, 8, stride=16), :]
         hys[f, 1] = w[pl.ds(0, 8, stride=16), :]
 
-    def send_halo(f, copies, planes):
+    def send_halo(f, planes):
         for d in DIRECTIONS:
             if planes != (d[2] != 0):
                 continue
-            k = DIRECTIONS.index(d)
+            rows = 1
             if d[2]:
                 j, side = (1 - d[0]) * 3 + (1 - d[1]), (1 - d[2]) // 2
                 source, target = hzs.at[f, j, pl.ds(side, 1)], hzr.at[f, side, pl.ds(j, 1)]
@@ -204,98 +208,86 @@
                 source, target = hes.at[f, e], her.at[f, e]
             elif d[0]:
                 source, target = hxs.at[f, (1 - d[0]) // 2], hx.at[f, (1 - d[0]) // 2]
+                rows = 16
             else:
                 source, target = hys.at[f, (1 - d[1]) // 2], hyr.at[f, (1 - d[1]) // 2]
-            copies[d] = remote(source, target, hss.at[f, k], hrs.at[f, k], near(d))
+                rows = 8
+            remote(source, target, halo_sem.at[f, 1 if planes else 0], near(d), rows)
 
     def start_halo(f, field):
-        copies = {}
         field = pack_planes(f, field)
-        send_halo(f, copies, True)
+        send_halo(f, True)
         pack_faces(f, field)
-        send_halo(f, copies, False)
-        return copies
-
-    def end_halo(f, copies):
+        send_halo(f, False)
+
+    def end_halo(f):
         w = work.at[f]
-        copies[0, 1, 0].wait_recv()
+        wait_rows(halo_sem.at[f, 0], 52)
         w[pl.ds(0, 8, stride=16), :] = w[pl.ds(0, 8, stride=16), :] + jnp.where(at_floor, 0.0, hyr[f, 0])
-        copies[0, -1, 0].wait_recv()
         w[pl.ds(15, 8, stride=16), :] = w[pl.ds(15, 8, stride=16), :] + jnp.where(at_ceiling, 0.0, hyr[f, 1])
-        copies[1, 0, 0].wait_recv()
         w[pl.ds(0, 16), :] = w[pl.ds(0, 16), :] + hx[f, 0]
-        copies[-1, 0, 0].wait_recv()
         w[pl.ds(112, 16), :] = w[pl.ds(112, 16), :] + hx[f, 1]
         for d in DIRECTIONS:
             if d[2] == 0 and d[0] and d[1]:
                 e = (1 - d[0]) + (1 - d[1]) // 2
                 row = (0 if d[0] == 1 else 112) + (0 if d[1] == 1 else 15)
-                copies[d].wait_recv()
                 cut = at_floor if d[1] == 1 else at_ceiling
                 w[pl.ds(row, 1), :] = w[pl.ds(row, 1), :] + jnp.where(cut, 0.0, her[f, e])
         field = w[...]
-        for d in reversed(DIRECTIONS):
-            if d[2]:
-                copies[d].wait_recv()
+        wait_rows(halo_sem.at[f, 1], 18)
         low = jnp.sum(jnp.where(z_keep, hzr[f, 0], 0.0), axis=0, keepdims=True)
         high = jnp.sum(jnp.where(z_keep, hzr[f, 1], 0.0), axis=0, keepdims=True)
         low = jnp.sum(jnp.where(eye, low, 0.0), axis=1, keepdims=True)
         high = jnp.sum(jnp.where(eye, high, 0.0), axis=1, keepdims=True)
         return field + jnp.where(lane_id == 0, low, 0.0) + jnp.where(lane_id == 127, high, 0.0)
 
-    def start_x(c):
-        return (
-            remote(vel.at[c, pl.ds(112, 16)], vhx.at[c, 0], vss.at[c, 0], vrs.at[c, 0], at_x(1)),
-            remote(vel.at[c, pl.ds(0, 16)], vhx.at[c, 1], vss.at[c, 1], vrs.at[c, 1], at_x(-1)),
-        )
-
-    def mid_xy(c, copies):
-        w = work.at[3 + c]
-        w[...] = vel[c]
-        copies[0].wait_recv()
-        w[pl.ds(0, 16), :] = w[pl.ds(0, 16), :] + vhx[c, 0]
-        copies[1].wait_recv()
-        w[pl.ds(112, 16), :] = w[pl.ds(112, 16), :] + vhx[c, 1]
-        both = w[pl.ds(7, 8, stride=16), :] + w[pl.ds(8, 8, stride=16), :]
-        w[pl.ds(7, 8, stride=16), :] = both
-        w[pl.ds(8, 8, stride=16), :] = both
-        vys[c, 0] = w[pl.ds(15, 8, stride=16), :]
-        vys[c, 1] = w[pl.ds(0, 8, stride=16), :]
-        return (
-            remote(vys.at[c, 0], vyr.at[c, 0], vss.at[c, 2], vrs.at[c, 2], at_y(1)),
-            remote(vys.at[c, 1], vyr.at[c, 1], vss.at[c, 3], vrs.at[c, 3], at_y(-1)),
-        )
-
-    def mid_yz(c, copies):
-        w = work.at[3 + c]
-        copies[0].wait_recv()
-        w[pl.ds(0, 8, stride=16), :] = w[pl.ds(0, 8, stride=16), :] + jnp.where(at_floor, 0.0, vyr[c, 0])
-        copies[1].wait_recv()
-        w[pl.ds(15, 8, stride=16), :] = w[pl.ds(15, 8, stride=16), :] + jnp.where(at_ceiling, 0.0, vyr[c, 1])
-        field = w[...]
-        vzs[c, 0] = jnp.sum(jnp.where(eye, field[:, 127:128], 0.0), axis=0, keepdims=True)
-        vzs[c, 1] = jnp.sum(jnp.where(eye, field[:, 0:1], 0.0), axis=0, keepdims=True)
-        out = (
-            remote(vzs.at[c, 0], vzr.at[c, 0], vss.at[c, 4], vrs.at[c, 4], at_z(1)),
-            remote(vzs.at[c, 1], vzr.at[c, 1], vss.at[c, 5], vrs.at[c, 5], at_z(-1)),
-        )
-        w[...] = (
-            field
-            + jnp.where(low_z, pltpu.roll(field, 1, 1), 0.0)
-            + jnp.where(high_z, pltpu.roll(field, 127, 1), 0.0)
-        )
-        return out
-
-    def end_z(c, copies):
-        field = work[3 + c]
-        copies[0].wait_recv()
-        low = jnp.sum(jnp.where(eye, vzr[c, 0], 0.0), axis=1, keepdims=True)
-        copies[1].wait_recv()
-        high = jnp.sum(jnp.where(eye, vzr[c, 1], 0.0), axis=1, keepdims=True)
-        field = field + jnp.where(lane_id == 0, low, 0.0) + jnp.where(lane_id == 127, high, 0.0)
-        high = field.astype(BF16)
-        vhi[pl.ds(128 * c, 128), :] = high
-        vlo[pl.ds(128 * c, 128), :] = (field - high.astype(F32)).astype(BF16)
+    def start_x():
+        for c in range(3):
+            remote(vel.at[c, pl.ds(112, 16)], vhx.at[c, 0], velocity_sem.at[0], at_x(1), 16)
+            remote(vel.at[c, pl.ds(0, 16)], vhx.at[c, 1], velocity_sem.at[0], at_x(-1), 16)
+
+    def mid_xy():
+        wait_rows(velocity_sem.at[0], 96)
+        for c in range(3):
+            w = work.at[3 + c]
+            w[...] = vel[c]
+            w[pl.ds(0, 16), :] = w[pl.ds(0, 16), :] + vhx[c, 0]
+            w[pl.ds(112, 16), :] = w[pl.ds(112, 16), :] + vhx[c, 1]
+            both = w[pl.ds(7, 8, stride=16), :] + w[pl.ds(8, 8, stride=16), :]
+            w[pl.ds(7, 8, stride=16), :] = both
+            w[pl.ds(8, 8, stride=16), :] = both
+            vys[c, 0] = w[pl.ds(15, 8, stride=16), :]
+            vys[c, 1] = w[pl.ds(0, 8, stride=16), :]
+            remote(vys.at[c, 0], vyr.at[c, 0], velocity_sem.at[1], at_y(1), 8)
+            remote(vys.at[c, 1], vyr.at[c, 1], velocity_sem.at[1], at_y(-1), 8)
+
+    def mid_yz():
+        wait_rows(velocity_sem.at[1], 48)
+        for c in range(3):
+            w = work.at[3 + c]
+            w[pl.ds(0, 8, stride=16), :] = w[pl.ds(0, 8, stride=16), :] + jnp.where(at_floor, 0.0, vyr[c, 0])
+            w[pl.ds(15, 8, stride=16), :] = w[pl.ds(15, 8, stride=16), :] + jnp.where(at_ceiling, 0.0, vyr[c, 1])
+            field = w[...]
+            vzs[c, 0] = jnp.sum(jnp.where(eye, field[:, 127:128], 0.0), axis=0, keepdims=True)
+            vzs[c, 1] = jnp.sum(jnp.where(eye, field[:, 0:1], 0.0), axis=0, keepdims=True)
+            remote(vzs.at[c, 0], vzr.at[c, 0], velocity_sem.at[2], at_z(1), 1)
+            remote(vzs.at[c, 1], vzr.at[c, 1], velocity_sem.at[2], at_z(-1), 1)
+            w[...] = (
+                field
+                + jnp.where(low_z, pltpu.roll(field, 1, 1), 0.0)
+                + jnp.where(high_z, pltpu.roll(field, 127, 1), 0.0)
+            )
+
+    def end_z():
+        wait_rows(velocity_sem.at[2], 6)
+        for c in range(3):
+            field = work[3 + c]
+            low = jnp.sum(jnp.where(eye, vzr[c, 0], 0.0), axis=1, keepdims=True)
+            high = jnp.sum(jnp.where(eye, vzr[c, 1], 0.0), axis=1, keepdims=True)
+            field = field + jnp.where(lane_id == 0, low, 0.0) + jnp.where(lane_id == 127, high, 0.0)
+            high = field.astype(BF16)
+            vhi[pl.ds(128 * c, 128), :] = high
+            vlo[pl.ds(128 * c, 128), :] = (field - high.astype(F32)).astype(BF16)
 
     table = deriv_table()
 
@@ -333,11 +325,10 @@
     loads["src"].wait()
     pack_faces(0, pack_planes(0, src[...]))
     pl.semaphore_wait(barrier, len(DIRECTIONS) + len(RING_Y))
-    halo = {}
-    send_halo(0, halo, True)
-    send_halo(0, halo, False)
+    send_halo(0, True)
+    send_halo(0, False)
     loads["vel"].wait()
-    cvx = [start_x(c) for c in range(3)]
+    start_x()
 
     loads["coords"].wait()
     loads["owner"].wait()
@@ -363,27 +354,24 @@
     for g in range(GY):
         sendp[g] = packed[8 * g : 8 * g + 8, :]
 
-    to_owner = []
     for k in range(1, GY):
         peer = lax.rem(gy + k, GY)
-        to_owner.append(
-            remote(sendp.at[peer], recvp.at[gy], pss.at[0, k], prs.at[0, k], (gx, peer, gz))
-        )
+        remote(sendp.at[peer], recvp.at[gy], particle_sem.at[0], (gx, peer, gz), 8)
     recvp[gy] = sendp[gy]
 
-    cvy = [mid_xy(c, cvx[c]) for c in range(3)]
+    mid_xy()
     loads["ky"].wait()
     loads["kyt"].wait()
     loads["met"].wait()
     loads["scr"].wait()
-    v0 = end_halo(0, halo)
+    v0 = end_halo(0)
 
     image0 = operator(v0)
-    halo = start_halo(1, image0)
-    cvz = [mid_yz(c, cvy[c]) for c in range(3)]
-    v1 = end_halo(1, halo)
+    start_halo(1, image0)
+    mid_yz()
+    v1 = end_halo(1)
     image1 = operator(v1)
-    halo = start_halo(2, image1)
+    start_halo(2, image1)
     place_y = row_id % 16
     share_x = jnp.where((row_id < 16) | (row_id >= 112), 0.5, 1.0)
     edge_y = (place_y % 8 == 0) | (place_y % 8 == 7)
@@ -398,12 +386,10 @@
         ],
         axis=0,
     )
-    for c in range(3):
-        end_z(c, cvz[c])
+    end_z()
 
     loads["lsc"].wait()
-    for copy in to_owner:
-        copy.wait_recv()
+    wait_rows(particle_sem.at[0], 8 * (GY - 1))
     points = gll_points()
     node = iota((8, 128), 0)
 
@@ -450,14 +436,11 @@
 
     lax.fori_loop(0, GY // 2, sample_two, 0)
 
-    to_home = []
     for k in range(1, GY):
         peer = lax.rem(gy + k, GY)
-        to_home.append(
-            remote(sendv.at[peer], recvv.at[gy], pss.at[1, k], prs.at[1, k], (gx, peer, gz))
-        )
+        remote(sendv.at[peer], recvv.at[gy], particle_sem.at[1], (gx, peer, gz), 8)
     recvv[gy] = sendv[gy]
-    v2 = end_halo(2, halo)
+    v2 = end_halo(2)
 
     dx, dy, dz = gradients(v2)
     rows = jnp.concatenate(
@@ -481,25 +464,19 @@
     msg[0] = row
     here = gx * GZ + gz
     rxz[here] = row
-    copies = []
     for i in range(GX):
         for k in range(GZ):
             if i or k:
-                n = i * GZ + k
                 device = (lax.rem(gx + i, GX), gy, lax.rem(gz + k, GZ))
-                copies.append(remote(msg.at[0], rxz.at[here], ass.at[n], ars.at[n], device))
-    for copy in copies:
-        copy.wait_recv()
+                remote(msg.at[0], rxz.at[here], sum_sem.at[0], device, 1)
+    wait_rows(sum_sem.at[0], GX * GZ - 1)
     row = jnp.sum(rxz[...], axis=0)
     msg[1] = row
     ry[gy] = row
-    copies = []
     for k in range(1, GY):
-        n = GX * GZ + k
-        copies.append(remote(msg.at[1], ry.at[gy], ass.at[n], ars.at[n], at_y(k)))
-
-    for copy in to_home:
-        copy.wait_recv()
+        remote(msg.at[1], ry.at[gy], sum_sem.at[1], at_y(k), 1)
+
+    wait_rows(particle_sem.at[1], 8 * (GY - 1))
     back = jnp.concatenate([recvv[g] for g in range(GY)], axis=0)
     spread = jnp.dot(back, slots, precision=EXACT, preferred_element_type=F32)
     velocity = jnp.zeros((8, 512), F32)
@@ -507,8 +484,7 @@
         velocity = velocity + spread[8 * g : 8 * g + 8, :] * owned[g : g + 1, :]
     pv_out[...] = velocity[0:3, :]
 
-    for copy in copies:
-        copy.wait_recv()
+    wait_rows(sum_sem.at[1], GY - 1)
     row = jnp.sum(ry[...], axis=0)
 
     lane = iota((1, 128), 1)
@@ -545,8 +521,8 @@
         rr = new
     p_out[...] = (solution_row[0] * v0 + solution_row[1] * v1 + solution_row[2] * v2) * SCALE
 
-    for copy in sends:
-        copy.wait_send()
+    wait_rows(send_sem.at[0], sum(sent_rows))
+    assert sum(sent_rows) == SENT_ROWS
 
 
 def body(vel, src, met, scr, coords, owner, elem):
@@ -588,28 +564,26 @@
             pltpu.VMEM((3, 4, 1, 128), F32),
             pltpu.VMEM((3, 9, 2, 128), F32),
             pltpu.VMEM((3, 2, 16, 128), F32),
-            dma((3, 26)),
-            dma((3, 26)),
+            dma((3, 2)),
             pltpu.VMEM((3, 2, 16, 128), F32),
             pltpu.VMEM((3, 2, 8, 128), F32),
             pltpu.VMEM((3, 2, 8, 128), F32),
             pltpu.VMEM((3, 2, 1, 128), F32),
             pltpu.VMEM((3, 2, 1, 128), F32),
-            dma((3, 6)),
-            dma((3, 6)),
+            dma((3,)),
             pltpu.VMEM((2, 1, 128), F32),
             pltpu.VMEM((GX * GZ, 1, 128), F32),
             pltpu.VMEM((GY, 1, 128), F32),
-            dma((GX * GZ + GY,)),
-            dma((GX * GZ + GY,)),
+            dma((2,)),
             pltpu.VMEM((GY, 8, 128), F32),
             pltpu.VMEM((GY, 8, 128), F32),
             pltpu.VMEM((GY, 8, 128), F32),
             pltpu.VMEM((GY, 8, 128), F32),
-            dma((2, GY)),
-            dma((2, GY)),
+            dma((2,)),
             pltpu.VMEM((384, 128), BF16),
             pltpu.VMEM((384, 128), BF16),
+            dma((1,)),
+            pltpu.VMEM((SENT_ROWS, 1, 128), F32),
         ],
         compiler_params=pltpu.CompilerParams(collective_id=0, has_side_effects=True),
         name="step",

time: 47.9 us -> 44.6 us (0.931)
  Pallas kernels: 45.9 us -> 42.6 us
    pallas_call x1, Pallas kernels: 45.9 us -> 42.6 us  [body(): pl.pallas_call(kernel, out_shape=(pltpu.VMEM((128, 128), F32), pltpu.VMEM...]
where the time goes in v4:
time: 44.6 us; the launch traced here: 44.4 us
  Pallas kernels  42.6 us (96%)
  local copies, waits for them, and re-layouts  1.23 us (3%)
  between operations  0.64 us (1%)
    pallas_call x1, Pallas kernels, body(): pl.pallas_call(kernel, out_shape=(pltpu.VMEM((128, 128), F32), pltpu.VMEM...  42.6 us
    unnamed x2, local copies, waits for them, and re-layouts  1.23 us

profile of v4, /device:TPU:1, one launch (start us, length us, event | category | flops | bytes accessed | tf_op | source)
XLA Modules:
  0.0 44.4 jit_solution(18004225124347298518)
XLA Ops:
  0.6 42.6 %step.1 = (f32[128,128]{1,0:T(8,128)S(1)}, f32[3,512]{1,0:T(4,128)S(1)}) custom-call(f32[3,128,128]{2,1,0:T(8,128)} %bitcast.8, f32[128,128]{1,0:T(8,128)} %bitcast.10, f32[3,128,128]{2,1,0:T(8,128)} %bitcast.9, f32[128,128]{1,0:T(8,128)} %bitcast.11, f32[3,512]{1,0:T(4,128)} %coords_in.1, s32[1,512]{1,0:T(1,128)} %bitcast.12, s32[1,512]{1,0:T(1,128)} %bitcast.13, ...), custom_call_target="tpu_custom_call" | custom-call | tf_op jit(solution)/shard_map/step/pallas_call | solution.py:547
  43.2 0.6 %copy.14 = f32[8,16,128]{2,1,0:T(8,128)} copy(f32[8,16,128]{2,1,0:T(8,128)S(1)} %bitcast.7) | data formatting | bytes 131072
  43.8 0.6 %copy.15 = f32[3,512]{1,0:T(4,128)} copy(f32[3,512]{1,0:T(4,128)S(1)} %get-tuple-element.7) | data formatting | bytes 12288

commit v5 on v4

--- a/solution.py
+++ b/solution.py
@@ -74,7 +74,18 @@
     key=lambda d: -sum(abs(v) for v in d),
 )
 SENT_ROWS = 3 * 70 + 150 + 31 + 15 + 2 * 120
+FAR_XZ = sorted(
+    ((i, k) for i in range(GX) for k in range(GZ) if i or k),
+    key=lambda p: -min(p[0], GX - p[0]) - min(p[1], GZ - p[1]),
+)
+FAR_Y = sorted(range(1, GY), key=lambda k: -min(k, GY - k))
 RING_Y = [k for k in range(2, GY - 1)]
+
+
+def tree(values):
+    while len(values) > 1:
+        values = [a + b for a, b in zip(values[0::2], values[1::2])]
+    return values[0]
 
 
 def kernel(
@@ -158,13 +169,9 @@
 
     z_keep = source_mask()
 
+    in_y = lax.broadcasted_iota(jnp.int32, (2, 128), 1) % 16
+
     def pack_planes(f, field):
-        w = work.at[f]
-        w[...] = field
-        both = w[pl.ds(7, 8, stride=16), :] + w[pl.ds(8, 8, stride=16), :]
-        w[pl.ds(7, 8, stride=16), :] = both
-        w[pl.ds(8, 8, stride=16), :] = both
-        field = w[...]
         pair = jnp.concatenate(
             [
                 jnp.sum(jnp.where(eye, field[:, 127:128], 0.0), axis=0, keepdims=True),
@@ -172,11 +179,15 @@
             ],
             axis=0,
         )
+        pair = (
+            pair
+            + jnp.where(in_y == 7, pltpu.roll(pair, 127, 1), 0.0)
+            + jnp.where(in_y == 8, pltpu.roll(pair, 1, 1), 0.0)
+        )
         for dx in (-1, 0, 1):
             for dy in (-1, 0, 1):
                 shift = (16 * dx - 15 * dy) % 128
                 hzs[f, (1 - dx) * 3 + (1 - dy)] = pltpu.roll(pair, shift, 1) if shift else pair
-        return field
 
     def pack_faces(f, field):
         w = work.at[f]
@@ -186,12 +197,15 @@
             + jnp.where(high_z, pltpu.roll(field, 127, 1), 0.0)
         )
         w[...] = field
+        both = w[pl.ds(7, 8, stride=16), :] + w[pl.ds(8, 8, stride=16), :]
+        w[pl.ds(7, 8, stride=16), :] = both
+        w[pl.ds(8, 8, stride=16), :] = both
         for d in DIRECTIONS:
             if d[2] == 0 and d[0] and d[1]:
                 row = (112 if d[0] == 1 else 0) + (15 if d[1] == 1 else 0)
                 hes[f, (1 - d[0]) + (1 - d[1]) // 2] = field[row : row + 1, :]
-        hxs[f, 0] = field[112:128, :]
-        hxs[f, 1] = field[0:16, :]
+        hxs[f, 0] = w[pl.ds(112, 16), :]
+        hxs[f, 1] = w[pl.ds(0, 16), :]
         hys[f, 0] = w[pl.ds(15, 8, stride=16), :]
         hys[f, 1] = w[pl.ds(0, 8, stride=16), :]
 
@@ -215,7 +229,7 @@
             remote(source, target, halo_sem.at[f, 1 if planes else 0], near(d), rows)
 
     def start_halo(f, field):
-        field = pack_planes(f, field)
+        pack_planes(f, field)
         send_halo(f, True)
         pack_faces(f, field)
         send_halo(f, False)
@@ -323,7 +337,8 @@
 
     sendv[...] = jnp.zeros_like(sendv)
     loads["src"].wait()
-    pack_faces(0, pack_planes(0, src[...]))
+    pack_planes(0, src[...])
+    pack_faces(0, src[...])
     pl.semaphore_wait(barrier, len(DIRECTIONS) + len(RING_Y))
     send_halo(0, True)
     send_halo(0, False)
@@ -464,16 +479,14 @@
     msg[0] = row
     here = gx * GZ + gz
     rxz[here] = row
-    for i in range(GX):
-        for k in range(GZ):
-            if i or k:
-                device = (lax.rem(gx + i, GX), gy, lax.rem(gz + k, GZ))
-                remote(msg.at[0], rxz.at[here], sum_sem.at[0], device, 1)
+    for i, k in FAR_XZ:
+        device = (lax.rem(gx + i, GX), gy, lax.rem(gz + k, GZ))
+        remote(msg.at[0], rxz.at[here], sum_sem.at[0], device, 1)
     wait_rows(sum_sem.at[0], GX * GZ - 1)
-    row = jnp.sum(rxz[...], axis=0)
+    row = tree([rxz[k] for k in range(GX * GZ)])
     msg[1] = row
     ry[gy] = row
-    for k in range(1, GY):
+    for k in FAR_Y:
         remote(msg.at[1], ry.at[gy], sum_sem.at[1], at_y(k), 1)
 
     wait_rows(particle_sem.at[1], 8 * (GY - 1))
@@ -485,7 +498,7 @@
     pv_out[...] = velocity[0:3, :]
 
     wait_rows(sum_sem.at[1], GY - 1)
-    row = jnp.sum(ry[...], axis=0)
+    row = tree([ry[k] for k in range(GY)])
 
     lane = iota((1, 128), 1)
     m = [jnp.sum(jnp.where(lane == k, row, 0.0), axis=1, keepdims=True) for k in range(6)]
@@ -523,6 +536,17 @@
 
     wait_rows(send_sem.at[0], sum(sent_rows))
     assert sum(sent_rows) == SENT_ROWS
+
+
+def write_out(p_in, pv_in, p_out, pv_out, sem):
+    copies = [
+        pltpu.make_async_copy(p_in, p_out, sem.at[0]),
+        pltpu.make_async_copy(pv_in, pv_out, sem.at[1]),
+    ]
+    for copy in copies:
+        copy.start()
+    for copy in copies:
+        copy.wait()
 
 
 def body(vel, src, met, scr, coords, owner, elem):
@@ -588,6 +612,19 @@
         compiler_params=pltpu.CompilerParams(collective_id=0, has_side_effects=True),
         name="step",
     )(*operands)
+    pressure = pltpu.with_memory_space_constraint(pressure, pltpu.VMEM)
+    velocity = pltpu.with_memory_space_constraint(velocity, pltpu.VMEM)
+    pressure, velocity = pl.pallas_call(
+        write_out,
+        out_shape=(
+            jax.ShapeDtypeStruct((128, 128), F32),
+            jax.ShapeDtypeStruct((3, 512), F32),
+        ),
+        in_specs=[vmem, vmem],
+        out_specs=(anywhere, anywhere),
+        scratch_shapes=[dma((2,))],
+        name="write_out",
+    )(pressure, velocity)
     return pressure.reshape(8, 16, 128), velocity
 
 

time: 44.6 us -> 44 us (0.987)
  local copies, waits for them, and re-layouts: 1.23 us -> 0 us
  Pallas kernels: 42.6 us -> 43.2 us
    unnamed x2 -> x0, local copies, waits for them, and re-layouts: 1.23 us -> none
    pallas_call x0 -> x1, Pallas kernels: none -> 0.65 us  [body(): pl.pallas_call(write_out, out_shape=(jax.ShapeDtypeStruct((128, 128), F32...]
where the time goes in v5:
time: 44 us; the launch traced here: 43.8 us
  Pallas kernels  43.2 us (98%)
  between operations  0.64 us (1%)
    pallas_call x1, Pallas kernels, body(): pl.pallas_call(kernel, out_shape=(pltpu.VMEM((128, 128), F32), pltpu.VMEM...  42.5 us

profile of v5, /device:TPU:1, one launch (start us, length us, event | category | flops | bytes accessed | tf_op | source)
XLA Modules:
  0.0 43.8 jit_solution(3525522953561951374)
XLA Ops:
  0.6 42.5 %step.1 = (f32[128,128]{1,0:T(8,128)S(1)}, f32[3,512]{1,0:T(4,128)S(1)}) custom-call(f32[3,128,128]{2,1,0:T(8,128)} %bitcast.7, f32[128,128]{1,0:T(8,128)} %bitcast.9, f32[3,128,128]{2,1,0:T(8,128)} %bitcast.8, f32[128,128]{1,0:T(8,128)} %bitcast.10, f32[3,512]{1,0:T(4,128)} %coords_in.1, s32[1,512]{1,0:T(1,128)} %bitcast.11, s32[1,512]{1,0:T(1,128)} %bitcast.12, ...), custom_call_target="tpu_custom_call" | custom-call | tf_op jit(solution)/shard_map/step/pallas_call | solution.py:571
  43.2 0.7 %write_out.1 = (f32[128,128]{1,0:T(8,128)}, f32[3,512]{1,0:T(4,128)}) custom-call(f32[128,128]{1,0:T(8,128)S(1)} %get-tuple-element.6.p_in, f32[3,512]{1,0:T(4,128)S(1)} %get-tuple-element.7.pv_in), custom_call_target="tpu_custom_call" | custom-call | tf_op jit(solution)/shard_map/write_out/pallas_call | solution.py:617
